TPU v7x, 256 devices: a whole 4x4x8 slice. The times are simulated.
256 devices in a mesh: row: 32 (over y, z_lo, core), col: 8 (over z_hi, x).
Axes of the slice: x: 4, y: 4, z: 8 (z_hi: 2, z_lo: 4; z = z_hi * 4 + z_lo), core: 2. Of those that a mesh axis runs over, the one named last changes fastest.
Arguments:
- positions: float32 [3, 32, 8, 128], P(None, 'row', 'col'), may hold values from 0 to 12
- species: int32 [32, 8, 128], P('row', 'col'), may hold values from 0 to 5
- counts: int32 [32, 8, 128], P('row', 'col'), may hold values from 32 to 64
- neighbours: int32 [32, 8, 64, 128], P('row', 'col'), may hold values from 0 to 1151
- ghost_index: int32 [32, 8, 8, 128], P('row', 'col'), may hold values from 0 to 127
- wave_numbers: int32 [3, 1000], replicated, may hold values from -6 to 6, as said below
- embedding: float32 [6, 128], replicated, may hold values from -6 to 6
- w_radial: float32 [16, 128], replicated, may hold values from -1.5 to 1.5
- w_mix: float32 [128, 128], replicated, may hold values from -0.5 to 0.5
- w_read: float32 [128, 128], replicated, may hold values from -0.5 to 0.5
- w_out: float32 [128], replicated, may hold values from -0.5 to 0.5
- amplitude: float32 [128], replicated, may hold values from 10 to 100
- kernel_width: float32 [128], replicated, may hold values from 0.5 to 4
- filter_gain: float32 [1000, 128], replicated, may hold values from 0.1 to 1.9
Outputs:
- forces: float32 [3, 32, 8, 128], P(None, 'row', 'col')
- virial: float32 [3, 3], replicated
Inputs may be any that keep to these rules, and one draw needn't show every extreme that they name: `wave_numbers`: the first two rows lie in -6 to 6, the third in 1 to 6. `counts`: slots at or beyond an atom's count are padding. `neighbours`: indices into the extended table of step one. `ghost_index`: local atom indices; repeats are allowed.
All inputs are finite; a program needn't handle non-finite values.
Results may differ from a plain program's by a relative error of at most 0.0003.
Values sent between devices are 32-bit elements; how exact they have to be, the bound alone decides.
A program may use at most 64 MiB of HBM per device.

v0:
```python
import math

import jax
import jax.numpy as jnp
from jax import lax
from jax.sharding import PartitionSpec as P

CELL_EDGE = 12.0
HEIGHT = 36.0
EXACT = lax.Precision.HIGHEST
DIRECTIONS = ((-1, -1), (-1, 0), (-1, 1), (0, -1), (0, 1), (1, -1), (1, 0), (1, 1))


def with_halo(cells, sides, width):
    for axis, dim in sides:
        count = lax.axis_size(axis)
        head = lax.slice_in_dim(cells, 0, width, axis=dim)
        tail = lax.slice_in_dim(cells, cells.shape[dim] - width, cells.shape[dim], axis=dim)
        cells = jnp.concatenate(
            [
                lax.ppermute(tail, axis, [(i, (i + 1) % count) for i in range(count)]),
                cells,
                lax.ppermute(head, axis, [((i + 1) % count, i) for i in range(count)]),
            ],
            axis=dim,
        )
    return cells


def radial_rates(count):
    return 0.003 * jnp.exp(math.log(1.6) * jnp.arange(count, dtype=jnp.int32).astype(jnp.float32))


def block_size():
    return 125


def short_range(
    edge_vectors, own_kinds, edge_kinds, edge_valid, embedding, w_radial, w_mix, w_read, w_out
):
    slot_count, atom_count = edge_valid.shape
    species_count = embedding.shape[0]
    decay_rates = radial_rates(w_radial.shape[0])
    group_size = 4
    groups = slot_count // group_size
    vector_groups = jnp.moveaxis(edge_vectors.reshape(3, groups, group_size, atom_count), 1, 0)
    kind_groups = edge_kinds.reshape(groups, group_size, atom_count)
    mask_groups = edge_valid.reshape(groups, group_size, atom_count)
    species_ids = jnp.arange(species_count, dtype=jnp.int32)

    def one_group(running, inputs):
        vectors, neighbour_kinds, edge_mask = inputs
        squared = jnp.sum(vectors * vectors, axis=0)
        radial_basis = jnp.exp(-decay_rates[:, None, None] * squared[None])
        filters = jnp.einsum("rsa,rc->sac", radial_basis, w_radial, precision=EXACT)
        onehot = (neighbour_kinds[:, :, None] == species_ids[None, None, :]).astype(jnp.float32)
        features = jnp.einsum("sak,kc->sac", onehot, embedding, precision=EXACT)
        return (running + jnp.sum(edge_mask[:, :, None] * filters * features, axis=0), None)

    initial = jnp.zeros((atom_count, w_radial.shape[1]), jnp.float32)
    summed, _unused = lax.scan(
        jax.checkpoint(one_group), initial, (vector_groups, kind_groups, mask_groups)
    )
    aggregate = summed / slot_count
    own_onehot = (own_kinds[:, None] == species_ids[None, :]).astype(jnp.float32)
    initial_features = jnp.dot(own_onehot, embedding, precision=EXACT)
    updated = initial_features + jax.nn.silu(jnp.dot(aggregate, w_mix, precision=EXACT))
    readout = jax.nn.silu(jnp.dot(updated, w_read, precision=EXACT))
    energy = jnp.sum(jnp.dot(readout, w_out, precision=EXACT))
    return (energy, updated)


def structure_factors(coords, features, wave_vectors):
    wave_count = wave_vectors.shape[1]
    block_width = block_size()
    blocks = jnp.moveaxis(wave_vectors.reshape(3, wave_count // block_width, block_width), 1, 0)

    def one_block(wave_block):
        phases = jnp.einsum("xk,xn->kn", wave_block, coords, precision=EXACT)
        return jnp.stack(
            [
                jnp.dot(jnp.cos(phases), features, precision=EXACT),
                jnp.dot(jnp.sin(phases), features, precision=EXACT),
            ]
        )

    pieces = lax.map(jax.checkpoint(one_block), blocks)
    return jnp.moveaxis(pieces, 1, 0).reshape(2, wave_count, features.shape[1])


def wave_vectors_of(wave_numbers, row_count, col_count):
    lengths = jnp.array([CELL_EDGE * row_count, CELL_EDGE * col_count, HEIGHT], jnp.float32)
    return 2.0 * math.pi * wave_numbers.astype(jnp.float32) / lengths[:, None]


def spread_directions(payload):
    empty_cell = jnp.zeros_like(payload[:1])
    return jnp.concatenate([payload[:4], empty_cell, payload[4:]], axis=0).reshape(
        (3, 3) + payload.shape[1:]
    )


def gather_directions(padded):
    corner_cells = padded[0::2, 0::2]
    flattened = corner_cells.reshape((9,) + corner_cells.shape[2:])
    return jnp.concatenate([flattened[:4], flattened[5:]], axis=0)


def per_device(
    positions,
    species,
    counts,
    neighbours,
    ghost_index,
    wave_numbers,
    embedding,
    w_radial,
    w_mix,
    w_read,
    w_out,
    amplitude,
    kernel_width,
    filter_gain,
):
    own_coords = positions[:, 0, 0, :]
    own_kinds = species[0, 0]
    live_counts = counts[0, 0]
    neighbour_ids = neighbours[0, 0]
    ghost_list = ghost_index[0, 0]
    atom_count = own_kinds.shape[0]
    ghost_count = ghost_list.shape[1]
    direction_count = ghost_list.shape[0]
    slot_count = neighbour_ids.shape[0]
    sent_coords = jnp.moveaxis(own_coords[:, ghost_list], 1, 0)
    sent_kinds = own_kinds[ghost_list].astype(jnp.float32)[:, None, :]
    outgoing = spread_directions(jnp.concatenate([sent_coords, sent_kinds], axis=1))
    padded = with_halo(outgoing, (("row", 0), ("col", 1)), 1)
    incoming = gather_directions(padded)
    step_table = jnp.array(DIRECTIONS, jnp.float32) * CELL_EDGE
    shift_table = jnp.concatenate(
        [step_table, jnp.zeros((direction_count, 1), jnp.float32)], axis=1
    )
    ghost_coords = incoming[:, :3, :] + shift_table[:, :, None]
    ext_coords = jnp.concatenate(
        [own_coords, jnp.moveaxis(ghost_coords, 1, 0).reshape(3, -1)], axis=1
    )
    ext_kinds = jnp.concatenate([own_kinds, incoming[:, 3, :].reshape(-1).astype(jnp.int32)])
    edge_vectors = ext_coords[:, neighbour_ids] - own_coords[:, None, :]
    edge_kinds = ext_kinds[neighbour_ids]
    edge_valid = (jnp.arange(slot_count, dtype=jnp.int32)[:, None] < live_counts[None, :]).astype(
        jnp.float32
    )

    def local_short(vectors):
        return short_range(
            vectors, own_kinds, edge_kinds, edge_valid, embedding, w_radial, w_mix, w_read, w_out
        )

    (short_energy, updated), short_back = jax.vjp(local_short, edge_vectors)
    row_count = lax.axis_size("row")
    col_count = lax.axis_size("col")
    volume = CELL_EDGE * row_count * CELL_EDGE * col_count * HEIGHT
    domain_shift = jnp.stack(
        [
            lax.axis_index("row").astype(jnp.float32) * CELL_EDGE,
            lax.axis_index("col").astype(jnp.float32) * CELL_EDGE,
            jnp.zeros((), jnp.float32),
        ]
    )
    global_coords = own_coords + domain_shift[:, None]
    wave_vectors = wave_vectors_of(wave_numbers, row_count, col_count)
    local_factors, factor_back = jax.vjp(
        lambda coords, features: structure_factors(coords, features, wave_vectors),
        global_coords,
        updated,
    )
    unit_weight = jnp.ones((), jnp.float32)
    squared_norm = jnp.sum(wave_vectors * wave_vectors, axis=0)
    weights = (
        amplitude[None, :] * filter_gain * jnp.exp(-kernel_width[None, :] * squared_norm[:, None])
    )
    factors = lax.psum(local_factors, ("row", "col"))
    coefficients = weights[None] * factors / volume
    strain_terms = jnp.sum(kernel_width[None, None, :] * coefficients * factors, axis=(0, 2))
    kspace_virial = jnp.zeros((3, 3), jnp.float32)
    tail_virial = jnp.eye(3, dtype=jnp.float32) * (
        0.5 * jnp.sum(coefficients * factors)
    ) - jnp.einsum("xk,k,yk->xy", wave_vectors, strain_terms, wave_vectors, precision=EXACT)
    coord_grad, feature_grad = factor_back(coefficients)
    vector_grad = short_back((unit_weight, feature_grad))[0]
    table_size = ext_coords.shape[1]
    table_grad = (
        jnp.zeros((3, table_size), jnp.float32)
        .at[:, neighbour_ids.reshape(-1)]
        .add(vector_grad.reshape(3, -1))
    )
    own_grad = table_grad[:, :atom_count] - jnp.sum(vector_grad, axis=1) + coord_grad
    ghost_grad = jnp.moveaxis(
        table_grad[:, atom_count:].reshape(3, direction_count, ghost_count), 1, 0
    )
    returned = gather_directions(
        with_halo(spread_directions(ghost_grad), (("row", 0), ("col", 1)), 1)
    )
    own_grad = own_grad.at[:, ghost_list.reshape(-1)].add(
        jnp.moveaxis(returned, 1, 0).reshape(3, -1)
    )
    local_virial = kspace_virial - jnp.einsum(
        "xsa,ysa->xy", vector_grad, edge_vectors, precision=EXACT
    )
    virial = (lax.psum(local_virial, ("row", "col")) + tail_virial) / volume
    forces = -own_grad
    return (forces[:, None, None, :], virial)


def solution(mesh):
    return jax.shard_map(
        per_device,
        mesh=mesh,
        in_specs=(
            P(None, "row", "col", None),
            P("row", "col", None),
            P("row", "col", None),
            P("row", "col", None, None),
            P("row", "col", None, None),
            P(),
            P(),
            P(),
            P(),
            P(),
            P(),
            P(),
            P(),
            P(),
        ),
        out_specs=(P(None, "row", "col", None), P()),
        check_vma=False,
    )
```

profile of v0, /device:TPU:1, one launch (start us, length us, event | category | flops | bytes accessed | tf_op | source)
XLA Modules:
  0.0 589.6 jit_solution(2064801875474946482)
XLA Ops:
  7.3 0.9 copy.106
  8.2 0.7 fusion.82
  8.9 2.8 gather_fusion
  11.9 5.9 gather_fusion.1
  17.8 3.1 collective-permute-start
  21.9 2.1 collective-permute-done.1
  23.9 1.2 collective-permute-start.2
  25.1 7.3 %collective-permute-start.3 = (f32[5,1,4,128]{3,2,1,0:T(4,128)S(1)}, f32[5,1,4,128]{3,2,1,0:T(4,128)S(1)}, u32[]{:S(2)}, u32[]{:S(2)}) collective-permute-start(f32[5,1,4,128]{3,2,1,0:T(4,128)S(1)} %get-tuple-element.716), channel_id=1, source_target_pairs={{1,0},{2,1},{3,2},{4,3},{5,4},{6,5},{7,6},{0,7},{9,8},{10,9},{11,1... | collective-permute-start | bytes 30728 | tf_op jit(solution)/shard_map/ppermute | solution.py:23
  33.6 27.9 %gather_fusion.2 = f32[8192,3]{1,0:T(8,128)} fusion(f32[3,1152]{0,1:T(8,128)S(1)} %pad_maximum_fusion, s32[8192]{0:T(1024)S(1)} %fusion.67), kind=kCustom, calls=%fused_computation.2 | custom fusion | bytes 229376 | tf_op jit(solution)/shard_map/gather | solution.py:148
  61.5 2.8 copy.110
  64.5 45.5 %gather_fusion.3 = s32[8192]{0:T(1024)S(1)} fusion(s32[1152]{0:T(1024)S(1)} %pad_add_fusion, s32[8192]{0:T(1024)S(1)} %fusion.67), kind=kCustom, calls=%fused_computation.3 | custom fusion | bytes 98304 | tf_op jit(solution)/shard_map/gather | solution.py:149
  110.0 19.2 %while.57 = (s32[]{:T(128)}, f32[128,128]{1,0:T(8,128)S(1)}, f32[16,4,128]{2,1,0:T(4,128)S(1)}, f32[16,3,4,128]{3,2,1,0:T(4,128)S(1)}, f32[16,128]{1,0:T(8,128)S...) while((s32[]{:T(128)}, f32[128,128]{1,0:T(8,128)S(1)}, ...), condition=%wide.region_4.5_spmd.clone, body=%wide.region_1.0_spmd.clone.sunk | while | flops 17528384 | bytes 820467 | solution.py:61
  110.1 0.7 convolution_multiply_fusion.8
  112.5 0.7 convolution_multiply_fusion.8
  113.7 0.7 convolution_multiply_fusion.8
  114.9 0.7 convolution_multiply_fusion.8
  126.9 0.7 convolution_multiply_fusion.8
  129.8 9.5 %while.55 = (s32[]{:T(128)}, f32[8,2,125,128]{3,2,1,0:T(8,128)S(1)}, f32[8,3,125]{2,1,0:T(4,128)S(1)}, f32[3,128]{1,0:T(4,128)S(1)}, f32[128,128]{1,0:T(8,128)S(1)}, /*index=5*/s32[]{:T(128)}) while((s32[]{:T(128)}, f32[8,2,125,128]{3,2,1,0:T(8,128)S(1)}, f32[8,3,125]{2,1,0:T(4,128)S(1)}, f32[3,128]{1,0:T(4,128)S(1)}, ...), condition=%wide.region_6.7_spmd, body=%wide.region_5.6_spmd.sunk | while | flops 49760000 | bytes 717389 | solution.py:87
  139.3 1.1 reshape.237
  140.7 264.0 %all-reduce.3.cloned.1.call-done = f32[2,1000,128]{2,1,0:T(8,128)} async-done(((f32[2,1000,128]{2,1,0:T(8,128)}), f32[2,1000,128]{2,1,0:T(8,128)}) %all-reduce.3.cloned.1.call-update) | async-done | bytes 1024016 | tf_op jit(solution)/shard_map/psum | solution.py:182
  404.7 2.2 multiply_reduce_fusion.3
  406.9 15.1 %while.58 = (s32[]{:T(128)}, f32[3,128]{1,0:T(4,128)S(1)}, f32[128,128]{1,0:T(8,128)S(1)}, f32[8,3,125]{2,1,0:T(4,128)S(1)}, f32[8,2,125,128]{3,2,0,1:T(8,128)S(...) while((s32[]{:T(128)}, f32[3,128]{1,0:T(4,128)S(1)}, ...), condition=%wide.region_9.10_spmd.clone, body=%wide.region_8.9_spmd.clone.sunk | while | flops 99569920 | bytes 1569780 | solution.py:87
  422.6 15.3 %while.56 = (s32[]{:T(128)}, f32[128,128]{1,0:T(8,128)S(1)}, f32[16,3,4,128]{3,2,1,0:T(4,128)S(1)}, f32[16,3,4,128]{3,2,1,0:T(4,128)S(1)}, s32[16,4,128]{2,1,0:T...) while((s32[]{:T(128)}, f32[128,128]{1,0:T(8,128)S(1)}, ...), condition=%wide.region_13.14_spmd.clone, body=%wide.region_10.13_spmd.clone.sunk | while | flops 17473604 | bytes 652721 | solution.py:61
  438.0 2.6 copy.121
  440.6 44.5 %scatter_custom_fusion = f32[3,1152]{0,1:T(8,128)S(1)} fusion(s32[8192]{0:T(1024)S(1)} %bitcast.243, f32[8192,3]{1,0:T(8,128)} %copy.121, f32[]{:T(128)} %constant.154.clone.1), kind=kCustom, calls=%fused_computation.83 | custom fusion | flops 24576 | bytes 14336 | tf_op jit(solution)/shard_map/scatter-add | solution.py:195
  485.3 0.7 fusion.45
  486.1 77.6 %psum.15 = f32[3,3]{1,0:T(4,128)S(1)} all-reduce(f32[3,3]{1,0:T(4,128)S(1)} %fusion.45), channel_id=1, replica_groups=mesh['row'=32,'col'=8] {'row','col'}, use_global_device_ids=true, to_apply=%region_17.18 | all-reduce | flops 9 | bytes 72 | tf_op jit(solution)/shard_map/psum | solution.py:210
  565.1 0.8 fusion.44
  565.9 1.2 collective-permute-done.5
  567.5 7.1 %collective-permute-start.7 = (f32[5,1,3,128]{3,2,1,0:T(4,128)S(1)}, f32[5,1,3,128]{3,2,1,0:T(4,128)S(1)}, u32[]{:S(2)}, u32[]{:S(2)}) collective-permute-start(f32[5,1,3,128]{3,2,1,0:T(4,128)S(1)} %get-tuple-element.714), channel_id=1, source_target_pairs={{1,0},{2,1},{3,2},{4,3},{5,4},{6,5},{7,6},{0,7},{9,8},{10,9},{11,1... | collective-permute-start | bytes 23048 | tf_op jit(solution)/shard_map/ppermute | solution.py:23
  574.8 0.9 collective-permute-done.6
  576.0 6.1 %scatter_fusion = f32[3,128]{0,1:T(8,128)S(1)} fusion(f32[3,128]{0,1:T(8,128)S(1)} %copy.127, s32[1024]{0:T(1024)S(1)} %bitcast.244, f32[1024,3]{1,0:T(8,128)S(1)} %bitcast.225), kind=kCustom, calls=%fused_computation.5 | custom fusion | flops 3072 | bytes 40960 | tf_op jit(solution)/shard_map/scatter-add | solution.py:204
  (470 shorter events, 59.1 us)
Async XLA Ops:
  7.2 133.3 %copy-start = (f32[128,128]{1,0:T(8,128)S(1)}, f32[128,128]{1,0:T(8,128)}, u32[]{:S(2)}) copy-start(f32[128,128]{1,0:T(8,128)} %param.33) | copy-start | bytes 196612
  7.2 14.2 %copy-start.11 = (f32[3]{0:T(128)S(1)}, f32[3]{0:T(128)}, u32[]{:S(2)}) copy-start(f32[3]{0:T(128)} %constant.180) | copy-start | bytes 40
  7.2 26.1 %copy-start.9 = (f32[8,3]{1,0:T(8,128)S(1)}, f32[8,3]{1,0:T(8,128)}, u32[]{:S(2)}) copy-start(f32[8,3]{1,0:T(8,128)} %constant.182) | copy-start | bytes 292
  7.2 14.0 %copy-start.5 = (s32[1,1,64,128]{3,2,1,0:T(8,128)S(1)}, s32[1,1,64,128]{3,2,1,0:T(8,128)}, u32[]{:S(2)}) copy-start(s32[1,1,64,128]{3,2,1,0:T(8,128)} %param.27) | copy-start | bytes 98308
  7.2 14.1 %copy-start.13 = (f32[128]{0:T(128)S(1)}, f32[128]{0:T(128)}, u32[]{:S(2)}) copy-start(f32[128]{0:T(128)} %param.36) | copy-start | bytes 1540
  7.2 14.2 %copy-start.7 = (s32[3,1000]{1,0:T(4,128)S(1)}, s32[3,1000]{1,0:T(4,128)}, u32[]{:S(2)}) copy-start(s32[3,1000]{1,0:T(4,128)} %param.29) | copy-start | bytes 36004
  7.2 14.4 %copy-start.10 = (f32[128]{0:T(128)S(1)}, f32[128]{0:T(128)}, u32[]{:S(2)}) copy-start(f32[128]{0:T(128)} %param.35) | copy-start | bytes 1540
  7.2 14.4 %copy-start.3 = (f32[1000,128]{1,0:T(8,128)S(1)}, f32[1000,128]{1,0:T(8,128)}, u32[]{:S(2)}) copy-start(f32[1000,128]{1,0:T(8,128)} %param.37) | copy-start | bytes 1536004
  7.3 25.1 %copy-start.12 = (s32[1,1,128]{2,1,0:T(1,128)S(1)}, s32[1,1,128]{2,1,0:T(1,128)}, u32[]{:S(2)}) copy-start(s32[1,1,128]{2,1,0:T(1,128)} %param.26) | copy-start | bytes 1540
  7.3 397.4 %all-reduce.3.cloned.1.call-start = ((), (), s32[]{:S(2)}) async-start(), calls=%async_computation | async-start | bytes 2048000 | tf_op jit(solution)/shard_map/psum | solution.py:182
  17.8 4.1 collective-permute-start
  20.9 3.1 collective-permute-start.1
  21.8 42.6 %copy-start.1 = (s32[1,1,128]{2,1,0:T(1,128)S(1)}, s32[1,1,128]{2,1,0:T(1,128)}, u32[]{:S(2)}) copy-start(s32[1,1,128]{2,1,0:T(1,128)} %param.25) | copy-start | bytes 1540
  23.9 9.3 %collective-permute-start.2 = (f32[5,1,4,128]{3,2,1,0:T(4,128)S(1)}, f32[5,1,4,128]{3,2,1,0:T(4,128)S(1)}, u32[]{:S(2)}, u32[]{:S(2)}) collective-permute-start(f32[5,1,4,128]{3,2,1,0:T(4,128)S(1)} %get-tuple-element.715), channel_id=1, source_target_pairs={{0,1},{1,2},{2,3},{3,4},{4,5},{5,6},{6,7},{7,0},{8,9},{9,10},{10,1... | collective-permute-start | bytes 30728 | tf_op jit(solution)/shard_map/ppermute | solution.py:21
  25.1 8.1 %collective-permute-start.3 = (f32[5,1,4,128]{3,2,1,0:T(4,128)S(1)}, f32[5,1,4,128]{3,2,1,0:T(4,128)S(1)}, u32[]{:S(2)}, u32[]{:S(2)}) collective-permute-start(f32[5,1,4,128]{3,2,1,0:T(4,128)S(1)} %get-tuple-element.716), channel_id=1, source_target_pairs={{1,0},{2,1},{3,2},{4,3},{5,4},{6,5},{7,6},{0,7},{9,8},{10,9},{11,1... | collective-permute-start | bytes 30728 | tf_op jit(solution)/shard_map/ppermute | solution.py:23
  64.4 45.6 %copy-start.2 = (f32[16,128]{1,0:T(8,128)S(1)}, f32[16,128]{1,0:T(8,128)}, u32[]{:S(2)}) copy-start(f32[16,128]{1,0:T(8,128)} %param.31) | copy-start | bytes 24580
  64.5 45.6 %copy-start.4 = (f32[6,128]{1,0:T(8,128)S(1)}, f32[6,128]{1,0:T(8,128)}, u32[]{:S(2)}) copy-start(f32[6,128]{1,0:T(8,128)} %param.30) | copy-start | bytes 9220
  110.0 19.3 %copy-start.6 = (f32[128,128]{1,0:T(8,128)S(1)}, f32[128,128]{1,0:T(8,128)}, u32[]{:S(2)}) copy-start(f32[128,128]{1,0:T(8,128)} %param.32) | copy-start | bytes 196612
  129.8 10.7 %copy-start.8 = (s32[1,1,8,128]{3,2,1,0:T(8,128)S(1)}, s32[1,1,8,128]{3,2,1,0:T(8,128)}, u32[]{:S(2)}) copy-start(s32[1,1,8,128]{3,2,1,0:T(8,128)} %param.28) | copy-start | bytes 12292
  406.9 15.1 %copy-start.14 = (f32[128]{0:T(128)S(1)}, f32[128]{0:T(128)}, u32[]{:S(2)}) copy-start(f32[128]{0:T(128)} %param.34) | copy-start | bytes 1540
  563.7 2.2 collective-permute-start.4
  564.1 3.1 collective-permute-start.5
  567.2 8.5 %collective-permute-start.6 = (f32[5,1,3,128]{3,2,1,0:T(4,128)S(1)}, f32[5,1,3,128]{3,2,1,0:T(4,128)S(1)}, u32[]{:S(2)}, u32[]{:S(2)}) collective-permute-start(f32[5,1,3,128]{3,2,1,0:T(4,128)S(1)} %get-tuple-element.713), channel_id=1, source_target_pairs={{0,1},{1,2},{2,3},{3,4},{4,5},{5,6},{6,7},{7,0},{8,9},{9,10},{10,1... | collective-permute-start | bytes 23048 | tf_op jit(solution)/shard_map/ppermute | solution.py:21
  567.5 8.2 %collective-permute-start.7 = (f32[5,1,3,128]{3,2,1,0:T(4,128)S(1)}, f32[5,1,3,128]{3,2,1,0:T(4,128)S(1)}, u32[]{:S(2)}, u32[]{:S(2)}) collective-permute-start(f32[5,1,3,128]{3,2,1,0:T(4,128)S(1)} %get-tuple-element.714), channel_id=1, source_target_pairs={{1,0},{2,1},{3,2},{4,3},{5,4},{6,5},{7,6},{0,7},{9,8},{10,9},{11,1... | collective-permute-start | bytes 23048 | tf_op jit(solution)/shard_map/ppermute | solution.py:23
Sparse Core Ops, SparseCore 0:
  140.5 264.0 all-reduce.2
where the time goes:
time: 598 us; the launch traced here: 590 us
  waiting for transfers between devices  269 us (45%)
  local copies, waits for them, and re-layouts  92.9 us (16%)
  blocking collectives  77.6 us (13%)
  matrix products  56.2 us (9%)
  other arithmetic  55.9 us (9%)
  starting transfers between devices  20 us (3%)
  between operations  15.3 us (3%)
    psum x1, waiting for transfers between devices, per_device(): factors = lax.psum(local_factors, ('row', 'col'))  264 us
    psum x1, blocking collectives, per_device(): virial = (lax.psum(local_virial, ('row', 'col')) + tail_virial) / volume  77.6 us
    gather x1, local copies, waits for them, and re-layouts, per_device(): edge_kinds = ext_kinds[neighbour_ids]  45.5 us
    scatter-add x1, other arithmetic, per_device(): table_grad = jnp.zeros((3, table_size), jnp.float32).at[:, neighbour_ids....  44.5 us
    gather x2, local copies, waits for them, and re-layouts, per_device(): edge_vectors = ext_coords[:, neighbour_ids] - own_coords[:, None, :]  30.7 us
    dot_general x32, matrix products, one_group(): filters = jnp.einsum('rsa,rc->sac', radial_basis, w_radial, precision=EXACT)  16.1 us
    ppermute x4, starting transfers between devices, with_halo(): lax.ppermute(head, axis, [((i + 1) % count, i) for i in range(count)])  14.9 us
    dot_general x32, matrix products, one_group(): features = jnp.einsum('sak,kc->sac', onehot, embedding, precision=EXACT)  14 us
  transfers between devices with their start and end apart: 9, of which 5 were waited for; matrix products, arithmetic and copies ran while one was open for 0% of the time, Pallas kernels for 0%

commit v1 on v0

v1 whole, which is shorter than its diff:
```python
import functools
import math

import jax
import jax.numpy as jnp
from jax import lax
from jax.experimental import pallas as pl
from jax.experimental.pallas import tpu as pltpu
from jax.sharding import PartitionSpec as P

CELL_EDGE = 12.0
HEIGHT = 36.0
ROWS = 32
COLS = 8
VOLUME = CELL_EDGE * ROWS * CELL_EDGE * COLS * HEIGHT
LENGTHS = (CELL_EDGE * ROWS, CELL_EDGE * COLS, HEIGHT)
DIRECTIONS = ((-1, -1), (-1, 0), (-1, 1), (0, -1), (0, 1), (1, -1), (1, 0), (1, 1))
RATE = 0.003
GROWTH = 1.6
BASIS = 16
SPECIES = 6
SLOTS = 64
WAVES = 1000
HIGH = lax.Precision.HIGH
HIGHEST = lax.Precision.HIGHEST
MESH = pl.DeviceIdType.MESH
F32 = jnp.float32
BF16 = jnp.bfloat16
SINE = (
    6.2831854820251465,
    -41.34170150756836,
    81.60513305664062,
    -76.70301818847656,
    42.02592849731445,
    -14.899847030639648,
    3.2381374835968018,
)
COSINE = (
    1.0,
    -19.73920440673828,
    64.93911743164062,
    -85.45014190673828,
    60.16762924194336,
    -25.967599868774414,
    6.528658390045166,
)
N_COPIES = 90


def dot(a, b, ca, cb, precision=None):
    return lax.dot_general(
        a, b, (((ca,), (cb,)), ((), ())), precision=precision, preferred_element_type=F32
    )


def horner(coefs, w):
    value = jnp.full_like(w, coefs[-1])
    for c in coefs[-2::-1]:
        value = value * w + c
    return value


def halves(x):
    hi = x.astype(BF16)
    lo = (x - hi.astype(F32)).astype(BF16)
    return hi, lo


def iota(shape, dim):
    return lax.broadcasted_iota(jnp.int32, shape, dim)


def kernel(
    pos, spec, cnt, nbr, gidx, wn, emb, wrad, wmix, wread, wout, amp, width, gain,
    force, virial,
    own, gsend, pages, gback, gret,
    nmat, umat, tab, emb8, w2,
    vec, kinds, dist, expo, basis, upd, dsilu, gshort,
    fsend, core_in, sums, in_a, in_b, part_a, part_b, in_a2, in_b2, zin, zbuf,
    c3, c2a, c2b, coef, fgrad, cgrad, vgrad, tgrad, vz, vy, vx, vq, vtile,
    ssem, rsem,
):
    row = lax.axis_index("row")
    col = lax.axis_index("col")
    q = lax.rem(row, 2)
    zl = lax.rem(lax.div(row, 2), 4)
    y = lax.div(row, 8)
    x = lax.rem(col, 4)
    zh = lax.div(col, 4)
    z = zh * 4 + zl

    def device(q, x, y, z):
        return (y * 8 + lax.rem(z, 4) * 2 + q, lax.div(z, 4) * 4 + x)

    ghosts = [
        (lax.rem(row + a + ROWS, ROWS), lax.rem(col + b + COLS, COLS)) for a, b in DIRECTIONS
    ]
    partner = device(1 - q, x, y, z)

    def along_x(off):
        return device(q, lax.rem(x + off, 4), y, z)

    def along_y(off):
        return device(q, x, lax.rem(y + off, 4), z)

    def along_z(off):
        return device(q, x, y, lax.rem(z + off, 8))

    def before(i, off, n):
        return lax.rem(i + n - off, n)

    def after(i, off, n):
        return lax.rem(i + off, n)

    barrier = pltpu.get_barrier_semaphore()
    greeted = (
        ghosts
        + [partner]
        + [along_x(off) for off in (1, 2, 3)]
        + [along_y(off) for off in (1, 2, 3)]
        + [along_z(off) for off in range(1, 8)]
    )
    for who in greeted:
        pl.semaphore_signal(barrier, inc=1, device_id=who, device_id_type=MESH)

    started = []

    def send(src, dst, landing, who):
        i = len(started)
        copy = pltpu.make_async_remote_copy(
            src_ref=src,
            dst_ref=dst,
            send_sem=ssem.at[i],
            recv_sem=rsem.at[i],
            device_id=who,
            device_id_type=MESH,
        )
        copy.start()
        started.append(copy)
        return pltpu.make_async_remote_copy(
            src_ref=src,
            dst_ref=landing,
            send_sem=ssem.at[i],
            recv_sem=rsem.at[i],
            device_id=who,
            device_id_type=MESH,
        )

    own[...] = jnp.zeros((8, 128), F32)
    for d in range(3):
        own[d : d + 1, :] = pos[d, 0]
    own[3:4, :] = spec[0].astype(F32)
    table = own[...]
    for d in range(8):
        index = jnp.broadcast_to(gidx[0, 0, d : d + 1, :], (8, 128))
        gsend[d] = jnp.take_along_axis(table, index, axis=1, mode="promise_in_bounds")
    pages[0] = table

    pl.semaphore_wait(barrier, len(greeted))
    waits = [
        send(gsend.at[d], pages.at[8 - d], pages.at[8 - d], ghosts[d]) for d in range(8)
    ]

    gback[...] = jnp.zeros((8, 8, 128), F32)
    nmat[...] = jnp.zeros((16, 1024), F32)
    numbers = wn[...].astype(F32)
    for part in range(3):
        nmat[3 * part : 3 * part + 3, 0:WAVES] = numbers
    umat[...] = jnp.zeros((16, 128), F32)
    offset = (row.astype(F32) * CELL_EDGE, col.astype(F32) * CELL_EDGE, 0.0)
    for d in range(3):
        turn = (pos[d, 0] + offset[d]) * (1.0 / LENGTHS[d])
        for part in range(3):
            piece = turn.astype(BF16).astype(F32)
            umat[3 * part + d : 3 * part + d + 1, :] = piece
            turn = turn - piece
    fractions = umat[...].astype(BF16)

    def trig(i, carry):
        at = pl.multiple_of(i * 128, 128)
        block = nmat[:, pl.ds(at, 128)].astype(BF16)
        turns = dot(block, fractions, 0, 0)
        turns = turns - jnp.floor(turns + 0.5)
        w = turns * turns
        tab[0, pl.ds(at, 128), :] = horner(COSINE, w)
        tab[1, pl.ds(at, 128), :] = horner(SINE, w) * turns
        return carry

    lax.fori_loop(0, 8, trig, 0)
    emb8[...] = jnp.zeros((8, 128), F32)
    emb8[0:SPECIES, :] = emb[...]
    kinds8 = emb8[...]
    for r in range(BASIS):
        w2[8 * r : 8 * r + 8, :] = wrad[r : r + 1, :] * kinds8 * (1.0 / SLOTS)
    onehot = (spec[0] == iota((8, 128), 0)).astype(F32)
    start = dot(onehot, kinds8, 0, 0, HIGHEST)

    for w in waits:
        w.wait_recv()
    live = cnt[0]
    rows8 = iota((8, 128), 0)

    def edge(g, carry):
        at = pl.multiple_of(g * 8, 8)
        index = nbr[0, 0, pl.ds(at, 8), :]
        page = lax.shift_right_logical(index, 7)
        lane = lax.bitwise_and(index, 127)
        picked = [jnp.zeros((8, 128), F32)] * 4
        for p in range(9):
            here = page == p
            for d in range(4):
                line = pages[p, d : d + 1, :]
                if p > 0 and d < 2 and DIRECTIONS[p - 1][d]:
                    line = line + CELL_EDGE * DIRECTIONS[p - 1][d]
                found = jnp.take_along_axis(
                    jnp.broadcast_to(line, (8, 128)), lane, axis=1, mode="promise_in_bounds"
                )
                picked[d] = jnp.where(here, found, picked[d])
        square = jnp.zeros((8, 128), F32)
        for d in range(3):
            v = picked[d] - pos[d, 0]
            vec[d, pl.ds(at, 8), :] = v
            square = square + v * v
        dist[pl.ds(at, 8), :] = square
        kinds[pl.ds(at, 8), :] = jnp.where(rows8 + at < live, picked[3], -1.0)
        return carry

    lax.fori_loop(0, 8, edge, 0)

    def radial(r, rate):
        e = jnp.exp(dist[...] * (-rate))
        expo[r] = e
        k = kinds[...]
        tile = jnp.zeros((8, 128), F32)
        for s in range(SPECIES):
            total = jnp.sum(jnp.where(k == s, e, 0.0), axis=0, keepdims=True)
            tile = jnp.where(rows8 == s, total, tile)
        basis[pl.ds(pl.multiple_of(r * 8, 8), 8), :] = tile
        return rate * GROWTH

    lax.fori_loop(0, BASIS, radial, jnp.float32(RATE))

    aggregate = dot(basis[...], w2[...], 0, 0, HIGH)
    u = dot(aggregate, wmix[...], 1, 0, HIGH)
    gate = 1.0 / (1.0 + jnp.exp(-u))
    upd[...] = start + u * gate
    dsilu[...] = gate * (1.0 + u * (1.0 - gate))

    def factor(half, i):
        return dot(tab[half, 128 * i : 128 * i + 128, :], upd[...], 1, 0, HIGH)

    waits = []
    for i in range(8):
        at = slice(128 * i, 128 * i + 128)
        fsend[at, :] = factor(1 - q, i)
        waits.append(send(fsend.at[at], core_in.at[at], core_in.at[at], partner))
    for i in range(8):
        at = slice(128 * i, 128 * i + 128)
        mine = factor(q, i)
        waits[i].wait_recv()
        sums[at, :] = mine + core_in[at, :]

    waits_a, waits_b = [], []
    for off in (2, 1, 3):
        at = pl.ds(pl.multiple_of(after(x, off, 4) * 128, 128), 128)
        waits_a.append(send(sums.at[at], in_a.at[off - 1], in_a.at[off - 1], along_x(off)))
        at = pl.ds(pl.multiple_of(512 + after(y, off, 4) * 128, 128), 128)
        waits_b.append(send(sums.at[at], in_b.at[off - 1], in_b.at[off - 1], along_y(off)))
    p = dot(upd[...], wread[...], 1, 0, HIGH)
    gate = 1.0 / (1.0 + jnp.exp(-p))
    gshort[...] = dot(wout[...] * (gate * (1.0 + p * (1.0 - gate))), wread[...], 1, 1, HIGH)

    for w in waits_a:
        w.wait_recv()
    part_a[...] = sums[pl.ds(pl.multiple_of(x * 128, 128), 128), :] + in_a[0] + in_a[1] + in_a[2]
    waits_a2, waits_b2 = [], []
    for off in (2, 1, 3):
        at = pl.ds(pl.multiple_of(after(y, off, 4) * 32, 32), 32)
        waits_a2.append(send(part_a.at[at], in_a2.at[off - 1], in_a2.at[off - 1], along_y(off)))
    for w in waits_b:
        w.wait_recv()
    part_b[...] = (
        sums[pl.ds(pl.multiple_of(512 + y * 128, 128), 128), :] + in_b[0] + in_b[1] + in_b[2]
    )
    for off in (2, 1, 3):
        at = pl.ds(pl.multiple_of(after(x, off, 4) * 32, 32), 32)
        waits_b2.append(send(part_b.at[at], in_b2.at[off - 1], in_b2.at[off - 1], along_x(off)))
    for w in waits_a2:
        w.wait_recv()
    zbuf[0:32, :] = (
        part_a[pl.ds(pl.multiple_of(y * 32, 32), 32), :] + in_a2[0] + in_a2[1] + in_a2[2]
    )
    for w in waits_b2:
        w.wait_recv()
    zbuf[32:64, :] = (
        part_b[pl.ds(pl.multiple_of(x * 32, 32), 32), :] + in_b2[0] + in_b2[1] + in_b2[2]
    )
    waits = []
    for off in (4, 3, 5, 2, 6, 1, 7):
        at = pl.ds(pl.multiple_of(after(z, off, 8) * 8, 8), 8)
        waits.append(send(zbuf.at[at], zin.at[off - 1], zin.at[off - 1], along_z(off)))

    first = (1 - zh) * (128 * x + 32 * y) + zh * (512 + 128 * y + 32 * x) + 8 * zl
    chosen = (iota((8, 1024), 1) == iota((8, 1024), 0) + first).astype(BF16)
    mine = dot(chosen, nmat[...].astype(BF16), 1, 1)
    k_of = [mine[:, d : d + 1] * (2.0 * math.pi / LENGTHS[d]) for d in range(3)]
    norm = k_of[0] * k_of[0] + k_of[1] * k_of[1] + k_of[2] * k_of[2]
    inside = lax.div(first, WAVES)
    source = pl.multiple_of(first - inside * WAVES, 8)
    weight = amp[...] * gain[pl.ds(source, 8), :] * jnp.exp(-width[...] * norm)
    weight = jnp.where(rows8 + first < WAVES, weight * (1.0 / VOLUME), 0.0)

    for w in waits:
        w.wait_recv()
    total = zbuf[pl.ds(pl.multiple_of(z * 8, 8), 8), :]
    for i in range(7):
        total = total + zin[i]
    result = weight * total
    mine_z = pl.ds(pl.multiple_of(z * 8, 8), 8)
    c3[mine_z, :] = result
    waits = []
    for off in (4, 3, 5, 2, 6, 1, 7):
        at = pl.ds(pl.multiple_of(before(z, off, 8) * 8, 8), 8)
        waits.append(send(c3.at[mine_z], c3.at[mine_z], c3.at[at], along_z(off)))

    power = result * total
    strain = jnp.sum(width[...] * power, axis=1, keepdims=True)
    energy = 0.5 * jnp.sum(jnp.sum(power, axis=1, keepdims=True), axis=0, keepdims=True)
    rows_v = iota((8, 128), 0)
    lanes_v = iota((8, 128), 1)
    tile = jnp.where((rows_v == lanes_v) & (rows_v < 3), energy, 0.0)
    for a in range(3):
        for b in range(a, 3):
            s = jnp.sum(k_of[a] * k_of[b] * strain, axis=0, keepdims=True)
            there = (rows_v == a) & (lanes_v == b)
            if a != b:
                there = there | ((rows_v == b) & (lanes_v == a))
            tile = tile - jnp.where(there, s, 0.0)
    vtile[...] = tile

    fgrad[...] = gshort[...]
    cgrad[...] = jnp.zeros((16, 128), F32)

    for w in waits:
        w.wait_recv()
    waits_a, waits_b = [], []
    mine_a = pl.ds(pl.multiple_of(y * 32, 32), 32)
    mine_b = pl.ds(pl.multiple_of(x * 32, 32), 32)
    for off in (2, 1, 3):
        at = pl.ds(pl.multiple_of(before(y, off, 4) * 32, 32), 32)
        waits_a.append(send(c3.at[0:32], c2a.at[mine_a], c2a.at[at], along_y(off)))
        at = pl.ds(pl.multiple_of(before(x, off, 4) * 32, 32), 32)
        waits_b.append(send(c3.at[32:64], c2b.at[mine_b], c2b.at[at], along_x(off)))
    c2a[mine_a, :] = c3[0:32, :]
    c2b[mine_b, :] = c3[32:64, :]

    chunk_a = pl.ds(pl.multiple_of(x * 128, 128), 128)
    chunk_b = pl.ds(pl.multiple_of(512 + y * 128, 128), 128)
    arrivals = []
    for w in waits_a:
        w.wait_recv()
    for off in (2, 1, 3):
        at = pl.ds(pl.multiple_of(before(x, off, 4) * 128, 128), 128)
        arrivals.append((send(c2a, coef.at[q, chunk_a], coef.at[q, at], along_x(off)), at))
    shared = [(send(c2a, coef.at[q, chunk_a], coef.at[1 - q, chunk_a], partner), chunk_a)]
    coef[q, chunk_a, :] = c2a[...]
    for w in waits_b:
        w.wait_recv()
    for off in (2, 1, 3):
        at = pl.ds(pl.multiple_of(512 + before(y, off, 4) * 128, 128), 128)
        arrivals.append((send(c2b, coef.at[q, chunk_b], coef.at[q, at], along_y(off)), at))
    shared.append((send(c2b, coef.at[q, chunk_b], coef.at[1 - q, chunk_b], partner), chunk_b))
    coef[q, chunk_b, :] = c2b[...]

    def back(half, sign, at):
        c = coef[half, at, :]
        fgrad[...] += dot(tab[half, at, :], c, 0, 0, HIGH)
        turned = dot(c, upd[...], 1, 1, HIGH) * tab[1 - half, at, :] * sign
        cgrad[...] += dot(nmat[:, at], turned, 1, 0, HIGH)

    sign_q = (2 * q - 1).astype(F32)
    back(q, sign_q, chunk_a)
    back(q, sign_q, chunk_b)
    for i in (1, 4, 2, 5, 0, 3):
        w, at = arrivals[i]
        w.wait_recv()
        shared.append((send(coef.at[q, at], coef.at[q, at], coef.at[1 - q, at], partner), at))
        back(q, sign_q, at)
    for w, at in shared:
        w.wait_recv()
        back(1 - q, -sign_q, at)

    du = fgrad[...] * dsilu[...]
    daggregate = dot(du, wmix[...], 1, 1, HIGH)
    basis[...] = dot(w2[...], daggregate, 1, 1, HIGH)

    def radial_back(r, carry):
        rate, grad = carry
        d = basis[pl.ds(pl.multiple_of(r * 8, 8), 8), :] * (-2.0 * rate)
        k = kinds[...]
        chosen = jnp.zeros((SLOTS, 128), F32)
        for s in range(SPECIES):
            chosen = jnp.where(k == s, d[s : s + 1, :], chosen)
        return rate * GROWTH, grad + chosen * expo[r]

    _, slope = lax.fori_loop(
        0, BASIS, radial_back, (jnp.float32(RATE), jnp.zeros((SLOTS, 128), F32))
    )
    spent = []
    for d in range(3):
        g = slope * vec[d]
        vgrad[d] = g
        spent.append(jnp.sum(g, axis=0, keepdims=True))
    tile = vtile[...]
    for a in range(3):
        for b in range(a, 3):
            s = jnp.sum(vgrad[a] * vec[b], axis=0, keepdims=True)
            s = jnp.sum(s, axis=1, keepdims=True)
            there = (rows_v == a) & (lanes_v == b)
            if a != b:
                there = there | ((rows_v == b) & (lanes_v == a))
            tile = tile - jnp.where(there, s, 0.0)

    def gather(buffer, value, me, n, to):
        buffer[me] = value
        return [
            send(buffer.at[me], buffer.at[me], buffer.at[before(me, off, n)], to(off))
            for off in range(1, n)
        ]

    def add_up(buffer, n):
        value = buffer[0]
        for i in range(1, n):
            value = value + buffer[i]
        return value

    waits_v = gather(vz, tile, z, 8, along_z)

    rows16 = iota((16, 128), 0)
    rows128 = iota((128, 128), 0)

    def scatter(g, total):
        left, right = [], []
        for s in range(4):
            at = pl.ds(g * 4 + s, 1)
            index = nbr[0, 0, at, :]
            page = lax.shift_right_logical(index, 7)
            lane = lax.bitwise_and(index, 127)
            right.append((rows128 == lane).astype(F32).astype(BF16))
            lines = jnp.concatenate(
                [jnp.where(rows16 == page, vgrad[d, at, :], 0.0) for d in range(3)], axis=0
            )
            left.append(jnp.concatenate(halves(lines), axis=0))
        return total + dot(
            jnp.concatenate(left, axis=1), jnp.concatenate(right, axis=1), 1, 1
        )

    total = lax.fori_loop(0, SLOTS // 4, scatter, jnp.zeros((96, 128), F32))
    tgrad[...] = total[0:48, :] + total[48:96, :]
    for p in range(8):
        for d in range(3):
            gback[p, d : d + 1, :] = tgrad[16 * d + p + 1 : 16 * d + p + 2, :]
    waits_g = [send(gback.at[p], gret.at[7 - p], gret.at[7 - p], ghosts[p]) for p in range(8)]

    for w in waits_v:
        w.wait_recv()
    waits_v = gather(vy, add_up(vz, 8), y, 4, along_y)
    left, right = [], []
    for d in range(8):
        right.append((rows128 == gidx[0, 0, d : d + 1, :]).astype(F32).astype(BF16))
    for w in waits_v:
        w.wait_recv()
    waits_v = gather(vx, add_up(vy, 4), x, 4, along_x)
    for w in waits_g:
        w.wait_recv()
    for d in range(8):
        hi, lo = halves(jnp.concatenate([gret[d], jnp.zeros((8, 128), F32)], axis=0))
        left.append(jnp.concatenate([hi, lo], axis=0))
    back_home = dot(jnp.concatenate(left, axis=1), jnp.concatenate(right, axis=1), 1, 1)
    back_home = back_home[0:16, :] + back_home[16:32, :]
    moved = cgrad[...]
    for d in range(3):
        grad = (
            tgrad[16 * d : 16 * d + 1, :]
            - spent[d]
            + moved[d : d + 1, :] * (2.0 * math.pi / LENGTHS[d])
            + back_home[d : d + 1, :]
        )
        force[d, 0] = -grad
    for w in waits_v:
        w.wait_recv()
    waits_v = gather(vq, add_up(vx, 4), q, 2, lambda off: partner)
    for w in waits_v:
        w.wait_recv()
    virial[...] = (add_up(vq, 2) * (1.0 / VOLUME))[0:3, 0:3]
    for copy in started:
        copy.wait_send()


def scratch():
    shapes = [
        (8, 128), (8, 8, 128), (9, 8, 128), (8, 8, 128), (8, 8, 128),
        (16, 1024), (16, 128), (2, 1024, 128), (8, 128), (128, 128),
        (3, 64, 128), (64, 128), (64, 128), (16, 64, 128), (128, 128),
        (128, 128), (128, 128), (128, 128),
        (1024, 128), (1024, 128), (1024, 128), (3, 128, 128), (3, 128, 128),
        (128, 128), (128, 128), (3, 32, 128), (3, 32, 128), (7, 8, 128), (64, 128),
        (64, 128), (128, 128), (128, 128), (2, 1024, 128), (128, 128), (16, 128),
        (3, 64, 128), (48, 128), (8, 8, 128), (4, 8, 128), (4, 8, 128), (2, 8, 128),
        (8, 128),
    ]
    return [pltpu.VMEM(s, F32) for s in shapes] + [
        pltpu.SemaphoreType.DMA((N_COPIES,)),
        pltpu.SemaphoreType.DMA((N_COPIES,)),
    ]


def per_device(
    positions, species, counts, neighbours, ghost_index, wave_numbers, embedding,
    w_radial, w_mix, w_read, w_out, amplitude, kernel_width, filter_gain,
):
    whole = pl.BlockSpec(memory_space=pltpu.VMEM)
    return pl.pallas_call(
        kernel,
        out_shape=(
            jax.ShapeDtypeStruct(positions.shape, F32),
            jax.ShapeDtypeStruct((3, 3), F32),
        ),
        in_specs=[whole] * 14,
        out_specs=(whole, whole),
        scratch_shapes=scratch(),
        compiler_params=pltpu.CompilerParams(collective_id=0, has_side_effects=True),
        name="ewald",
    )(
        positions, species, counts, neighbours, ghost_index, wave_numbers, embedding,
        w_radial, w_mix, w_read, w_out.reshape(1, 128), amplitude.reshape(1, 128),
        kernel_width.reshape(1, 128), filter_gain,
    )


def solution(mesh):
    return jax.shard_map(
        per_device,
        mesh=mesh,
        in_specs=(
            P(None, "row", "col", None),
            P("row", "col", None),
            P("row", "col", None),
            P("row", "col", None, None),
            P("row", "col", None, None),
            P(), P(), P(), P(), P(), P(), P(), P(), P(),
        ),
        out_specs=(P(None, "row", "col", None), P()),
        check_vma=False,
    )
```

time: 598 us -> 71.6 us (0.12); the launches traced: 590 us -> 71.4 us
  waiting for transfers between devices: 269 us -> 0 us
  local copies, waits for them, and re-layouts: 92.9 us -> 1.76 us
  blocking collectives: 77.6 us -> 0 us
  Pallas kernels: 0 us -> 69 us
  matrix products: 56.2 us -> 0 us
  other arithmetic: 55.9 us -> 0 us
  starting transfers between devices: 20 us -> 0 us
  between operations: 15.3 us -> 0.66 us
    psum x1 -> x0, waiting for transfers between devices: 264 us -> none  [per_device(): factors = lax.psum(local_factors, ('row', 'col'))]
    gather x6 -> x0, local copies, waits for them, and re-layouts: 85.1 us -> none  [the longest x1 45.5 us: per_device(): edge_kinds = ext_kinds[neighbour_ids]]
    psum x1 -> x0, blocking collectives: 77.6 us -> none  [per_device(): virial = (lax.psum(local_virial, ('row', 'col')) + tail_virial) / volume]
    pallas_call x0 -> x1, Pallas kernels: none -> 69 us  [per_device(): pl.pallas_call(kernel, out_shape=(jax.ShapeDtypeStruct(positions.shape, F...]
    dot_general x143 -> x0, matrix products: 56.2 us -> none  [the longest x32 16.1 us: one_group(): filters = jnp.einsum('rsa,rc->sac', radial_basis, w_radial, precision=EXACT)]
    scatter-add x2 -> x0, other arithmetic: 50.5 us -> none  [the longest x1 44.5 us: per_device(): table_grad = jnp.zeros((3, table_size), jnp.float32).at[:, neighbour_ids....]
    ppermute x8 -> x0, starting transfers between devices: 20 us -> none  [the longest x4 14.9 us: with_halo(): lax.ppermute(head, axis, [((i + 1) % count, i) for i in range(count)])]
  transfers between devices with their start and end apart: 9 -> 0, of which waited for: 5 -> 0; matrix products, arithmetic and copies ran while one was open for 0% -> 0% of each run, Pallas kernels for 0% -> 0%
where the time goes in v1:
time: 71.6 us; the launch traced here: 71.4 us
  Pallas kernels  69 us (96%)
  local copies, waits for them, and re-layouts  1.76 us (2%)
    pallas_call x1, Pallas kernels, per_device(): pl.pallas_call(kernel, out_shape=(jax.ShapeDtypeStruct(positions.shape, F...  69 us
    unnamed x6, local copies, waits for them, and re-layouts  1.76 us

profile of v1, /device:TPU:1, one launch (start us, length us, event | category | flops | bytes accessed | tf_op | source)
XLA Modules:
  0.0 71.4 jit_solution(12005696483964422617)
XLA Ops:
  0.6 69.0 %ewald.1 = (f32[3,1,1,128]{3,2,1,0:T(1,128)}, f32[3,3]{1,0:T(4,128)}) custom-call(f32[3,1,1,128]{3,2,1,0:T(1,128)} %pos.1, s32[1,1,128]{2,1,0:T(1,128)} %spec.1, s32[1,1,128]{2,1,0:T(1,128)} %cnt.1, s32[1,1,64,128]{3,2,1,0:T(8,128)} %nbr.1, s32[1,1,8,128]{3,2,1,0:T(8,128)} %gidx.1, s32[3,1000]{1,0:T(4,128)} %wn.1, f32[6,128]{1,0:T(8,128)} %emb.1, ...), custom_call_target="tpu_custom_call" | custom-call | tf_op jit(solution)/shard_map/ewald/pallas_call | solution.py:523
  69.7 0.0 copy-start.1
  69.7 0.0 copy-start
  69.7 0.6 copy-done.1
  70.3 0.6 copy.18
  70.9 0.0 copy-done
  70.9 0.6 copy.19
Async XLA Ops:
  69.7 0.6 copy-start.1
  69.7 1.2 %copy-start = (f32[3,3]{1,0:T(4,128)S(1)}, f32[3,3]{1,0:T(4,128)}, u32[]{:S(2)}) copy-start(f32[3,3]{1,0:T(4,128)} %get-tuple-element.5) | copy-start | bytes 112

commit v2 on v1

v2 whole, which is shorter than its diff:
```python
import functools
import math

import jax
import jax.numpy as jnp
from jax import lax
from jax.experimental import pallas as pl
from jax.experimental.pallas import tpu as pltpu
from jax.sharding import PartitionSpec as P

CELL_EDGE = 12.0
HEIGHT = 36.0
ROWS = 32
COLS = 8
VOLUME = CELL_EDGE * ROWS * CELL_EDGE * COLS * HEIGHT
LENGTHS = (CELL_EDGE * ROWS, CELL_EDGE * COLS, HEIGHT)
DIRECTIONS = ((-1, -1), (-1, 0), (-1, 1), (0, -1), (0, 1), (1, -1), (1, 0), (1, 1))
RATE = 0.003
GROWTH = 1.6
BASIS = 16
SPECIES = 6
SLOTS = 64
WAVES = 1000
HIGH = lax.Precision.HIGH
HIGHEST = lax.Precision.HIGHEST
MESH = pl.DeviceIdType.MESH
F32 = jnp.float32
BF16 = jnp.bfloat16
SINE = (
    6.2831854820251465,
    -41.34170150756836,
    81.60513305664062,
    -76.70301818847656,
    42.02592849731445,
    -14.899847030639648,
    3.2381374835968018,
)
COSINE = (
    1.0,
    -19.73920440673828,
    64.93911743164062,
    -85.45014190673828,
    60.16762924194336,
    -25.967599868774414,
    6.528658390045166,
)
def dot(a, b, ca, cb, precision=None):
    return lax.dot_general(
        a, b, (((ca,), (cb,)), ((), ())), precision=precision, preferred_element_type=F32
    )


def horner(coefs, w):
    value = jnp.full_like(w, coefs[-1])
    for c in coefs[-2::-1]:
        value = value * w + c
    return value


def halves(x):
    hi = x.astype(BF16)
    lo = (x - hi.astype(F32)).astype(BF16)
    return hi, lo


def iota(shape, dim):
    return lax.broadcasted_iota(jnp.int32, shape, dim)


N_COPIES = 130
INPUTS = (
    ((3, 1, 1, 128), F32), ((1, 1, 128), jnp.int32), ((1, 1, 128), jnp.int32),
    ((1, 1, 64, 128), jnp.int32), ((1, 1, 8, 128), jnp.int32), ((3, 1000), jnp.int32),
    ((6, 128), F32), ((16, 128), F32), ((128, 128), F32), ((128, 128), F32), ((1, 128), F32),
    ((1, 128), F32), ((1, 128), F32), ((1000, 128), F32),
)
SCRATCH = (
    ("own", (8, 128), F32), ("mate", (8, 128), F32), ("gsend", (8, 8, 128), F32),
    ("pages", (9, 8, 128), F32), ("gback", (8, 8, 128), F32), ("gret", (8, 8, 128), F32),
    ("nmat", (16, 1024), F32), ("umat", (16, 256), F32), ("tab", (2, 4, 128, 256), F32),
    ("tsplit", (2, 4, 128, 768), BF16), ("tturn", (2, 4, 256, 384), BF16),
    ("emb8", (8, 128), F32), ("w2", (128, 128), F32),
    ("vec", (3, 64, 128), F32), ("kinds", (64, 128), F32), ("dist", (64, 128), F32),
    ("expo", (16, 64, 128), F32), ("basis", (128, 128), F32), ("upd", (256, 128), F32),
    ("usplit", (768, 128), BF16), ("uturn", (384, 256), BF16),
    ("dsilu", (128, 128), F32), ("gshort", (128, 128), F32),
    ("sums", (2, 4, 4, 32, 128), F32), ("in1", (2, 3, 4, 32, 128), F32),
    ("part", (2, 4, 32, 128), F32), ("in2", (2, 3, 32, 128), F32),
    ("zin", (7, 8, 128), F32), ("zbuf", (64, 128), F32), ("c3", (64, 128), F32),
    ("coef", (2, 4, 4, 32, 128), F32), ("fgrad", (256, 128), F32), ("cgrad", (16, 256), F32),
    ("xout", (144, 128), F32), ("xin", (144, 128), F32),
    ("marks", (16, 128, 512), BF16), ("gmarks", (128, 1024), BF16),
    ("vgrad", (3, 64, 128), F32), ("tgrad", (48, 128), F32),
    ("va", (16, 8, 128), F32), ("vb", (16, 8, 128), F32),
)


def kernel(*refs):
    ins, out = refs[:14], refs[14]
    here = refs[15:29]
    named = refs[29 : 29 + len(SCRATCH)]
    ssem, rsem, lsem = refs[29 + len(SCRATCH) :]
    (pos, spec, cnt, nbr, gidx, wn, emb, wrad, wmix, wread, wout, amp, width, gain) = here
    (
        own, mate, gsend, pages, gback, gret, nmat, umat, tab, tsplit, tturn, emb8, w2,
        vec, kinds, dist, expo, basis, upd, usplit, uturn, dsilu, gshort,
        sums, in1, part, in2, zin, zbuf, c3, coef, fgrad, cgrad, xout, xin,
        marks, gmarks, vgrad, tgrad, va, vb,
    ) = named
    row = lax.axis_index("row")
    col = lax.axis_index("col")
    q = lax.rem(row, 2)
    zl = lax.rem(lax.div(row, 2), 4)
    y = lax.div(row, 8)
    x = lax.rem(col, 4)
    zh = lax.div(col, 4)
    z = zh * 4 + zl

    def device(q, x, y, z):
        return (y * 8 + lax.rem(z, 4) * 2 + q, lax.div(z, 4) * 4 + x)

    ghosts = [
        (lax.rem(row + a + ROWS, ROWS), lax.rem(col + b + COLS, COLS)) for a, b in DIRECTIONS
    ]
    partner = device(1 - q, x, y, z)

    def along_x(off):
        return device(q, lax.rem(x + off, 4), y, z)

    def along_y(off):
        return device(q, x, lax.rem(y + off, 4), z)

    def along_z(off):
        return device(q, x, y, lax.rem(z + off, 8))

    m_zq = z * 2 + q
    m_xy = x * 4 + y

    def among_zq(off):
        m = lax.rem(m_zq + off, 16)
        return device(lax.rem(m, 2), x, y, lax.div(m, 2))

    def among_xy(off):
        m = lax.rem(m_xy + off, 16)
        return device(q, lax.div(m, 4), lax.rem(m, 4), z)

    def before(i, off, n):
        return lax.rem(i + n - off, n)

    def after(i, off, n):
        return lax.rem(i + off, n)

    barrier = pltpu.get_barrier_semaphore()
    greeted = (
        ghosts
        + [among_zq(off) for off in range(1, 16)]
        + [among_xy(off) for off in range(1, 16)]
    )
    for who in greeted:
        pl.semaphore_signal(barrier, inc=1, device_id=who, device_id_type=MESH)
    loads = [pltpu.make_async_copy(ins[i], here[i], lsem.at[i]) for i in range(14)]
    for copy in loads:
        copy.start()

    started = []

    def send(src, dst, landing, who):
        i = len(started)
        copy = pltpu.make_async_remote_copy(
            src_ref=src,
            dst_ref=dst,
            send_sem=ssem.at[i],
            recv_sem=rsem.at[i],
            device_id=who,
            device_id_type=MESH,
        )
        copy.start()
        started.append(copy)
        return pltpu.make_async_remote_copy(
            src_ref=src,
            dst_ref=landing,
            send_sem=ssem.at[i],
            recv_sem=rsem.at[i],
            device_id=who,
            device_id_type=MESH,
        )

    gback[...] = jnp.zeros((8, 8, 128), F32)
    nmat[...] = jnp.zeros((16, 1024), F32)
    umat[...] = jnp.zeros((16, 256), F32)
    emb8[...] = jnp.zeros((8, 128), F32)
    own[...] = jnp.zeros((8, 128), F32)
    for copy in loads:
        copy.wait()

    for d in range(3):
        own[d : d + 1, :] = pos[d, 0]
    own[3:4, :] = spec[0].astype(F32)
    table = own[...]
    for d in range(8):
        index = jnp.broadcast_to(gidx[0, 0, d : d + 1, :], (8, 128))
        gsend[d] = jnp.take_along_axis(table, index, axis=1, mode="promise_in_bounds")
    pages[0] = table
    numbers = wn[...].astype(F32)
    for p in range(3):
        nmat[3 * p : 3 * p + 3, 0:WAVES] = numbers

    pl.semaphore_wait(barrier, len(greeted))
    wait_mate = send(own, mate, mate, partner)
    waits = [
        send(gsend.at[d], pages.at[8 - d], pages.at[8 - d], ghosts[d]) for d in range(8)
    ]

    emb8[0:SPECIES, :] = emb[...]
    kinds8 = emb8[...]
    for r in range(BASIS):
        w2[8 * r : 8 * r + 8, :] = wrad[r : r + 1, :] * kinds8 * (1.0 / SLOTS)
    onehot = (spec[0] == iota((8, 128), 0)).astype(F32)
    start = dot(onehot, kinds8, 0, 0, HIGHEST)

    wait_mate.wait_recv()
    column = col.astype(F32) * CELL_EDGE
    offsets = (
        (row.astype(F32) * CELL_EDGE, column, 0.0),
        ((row + 1 - 2 * q).astype(F32) * CELL_EDGE, column, 0.0),
    )
    for side, ref in enumerate((own, mate)):
        for d in range(3):
            turn = (ref[d : d + 1, :] + offsets[side][d]) * (1.0 / LENGTHS[d])
            for p in range(3):
                piece = turn.astype(BF16).astype(F32)
                umat[3 * p + d : 3 * p + d + 1, 128 * side : 128 * side + 128] = piece
                turn = turn - piece
    fractions = umat[...].astype(BF16)

    def trig(i, carry):
        block = nmat[:, pl.ds(pl.multiple_of(q * 512 + i * 128, 128), 128)].astype(BF16)
        turns = dot(block, fractions, 0, 0)
        turns = turns - jnp.floor(turns + 0.5)
        w = turns * turns
        for f, value in enumerate((horner(COSINE, w), horner(SINE, w) * turns)):
            tab[f, i] = value
            hi, lo = halves(value)
            for side in range(2):
                mine = slice(128 * side, 128 * side + 128)
                for p, half in enumerate((hi, lo, hi)):
                    at = 384 * side + 128 * p
                    tsplit[f, i, :, at : at + 128] = half[:, mine]
        turns = dot(fractions, block, 0, 0)
        turns = turns - jnp.floor(turns + 0.5)
        w = turns * turns
        for f, value in enumerate((horner(COSINE, w), horner(SINE, w) * turns)):
            hi, lo = halves(value)
            for p, half in enumerate((hi, lo, hi)):
                tturn[f, i, :, 128 * p : 128 * p + 128] = half
        return carry

    lax.fori_loop(0, 4, trig, 0)

    for w in waits:
        w.wait_recv()
    live = cnt[0]
    rows8 = iota((8, 128), 0)

    def edge(g, carry):
        at = pl.multiple_of(g * 8, 8)
        index = nbr[0, 0, pl.ds(at, 8), :]
        page = lax.shift_right_logical(index, 7)
        lane = lax.bitwise_and(index, 127)
        picked = [jnp.zeros((8, 128), F32)] * 4
        for p in range(9):
            here = page == p
            for d in range(4):
                line = pages[p, d : d + 1, :]
                if p > 0 and d < 2 and DIRECTIONS[p - 1][d]:
                    line = line + CELL_EDGE * DIRECTIONS[p - 1][d]
                found = jnp.take_along_axis(
                    jnp.broadcast_to(line, (8, 128)), lane, axis=1, mode="promise_in_bounds"
                )
                picked[d] = jnp.where(here, found, picked[d])
        square = jnp.zeros((8, 128), F32)
        for d in range(3):
            v = picked[d] - pos[d, 0]
            vec[d, pl.ds(at, 8), :] = v
            square = square + v * v
        dist[pl.ds(at, 8), :] = square
        kinds[pl.ds(at, 8), :] = jnp.where(rows8 + at < live, picked[3], -1.0)
        return carry

    lax.fori_loop(0, 8, edge, 0)

    def radial(r, rate):
        e = jnp.exp(dist[...] * (-rate))
        expo[r] = e
        k = kinds[...]
        tile = jnp.zeros((8, 128), F32)
        for s in range(SPECIES):
            total = jnp.sum(jnp.where(k == s, e, 0.0), axis=0, keepdims=True)
            tile = jnp.where(rows8 == s, total, tile)
        basis[pl.ds(pl.multiple_of(r * 8, 8), 8), :] = tile
        return rate * GROWTH

    lax.fori_loop(0, BASIS, radial, jnp.float32(RATE))

    aggregate = dot(basis[...], w2[...], 0, 0, HIGH)
    u = dot(aggregate, wmix[...], 1, 0, HIGH)
    gate = 1.0 / (1.0 + jnp.exp(-u))
    mine = start + u * gate
    upd[0:128, :] = mine
    wait_mate = send(upd.at[0:128], upd.at[128:256], upd.at[128:256], partner)
    dsilu[...] = gate * (1.0 + u * (1.0 - gate))
    p = dot(mine, wread[...], 1, 0, HIGH)
    gate = 1.0 / (1.0 + jnp.exp(-p))
    gshort[...] = dot(wout[...] * (gate * (1.0 + p * (1.0 - gate))), wread[...], 1, 1, HIGH)

    def split(side):
        value = upd[128 * side : 128 * side + 128, :]
        hi, lo = halves(value)
        for p, half in enumerate((hi, hi, lo)):
            usplit[384 * side + 128 * p : 384 * side + 128 * p + 128, :] = half
        hi, lo = halves(value.T)
        for p, half in enumerate((hi, hi, lo)):
            uturn[128 * p : 128 * p + 128, 128 * side : 128 * side + 128] = half

    split(0)
    wait_mate.wait_recv()
    split(1)

    place = (x, y)
    second = (y, x)
    along = (along_x, along_y)
    order = (2, 1, 3, 0)
    waits1 = {}
    for off in order:
        for f in range(2):
            chunk = after(place[f], off, 4)
            value = dot(tsplit[f, chunk], usplit[...], 1, 0)
            sums[f, chunk] = value.reshape(4, 32, 128)
            if off == 0:
                continue
            for off2 in order:
                waits1[f, off, off2] = send(
                    sums.at[f, chunk, after(second[f], off2, 4)],
                    in1.at[f, off - 1, off2],
                    in1.at[f, off - 1, off2],
                    along[f](off),
                )
    waits2 = {}
    for off2 in order:
        for f in range(2):
            for off in (1, 3, 2):
                waits1[f, off, off2].wait_recv()
            total = (
                sums[f, place[f], after(second[f], off2, 4)]
                + in1[f, 0, off2]
                + in1[f, 1, off2]
                + in1[f, 2, off2]
            )
            if off2 == 0:
                zbuf[32 * f : 32 * f + 32, :] = total
                continue
            part[f, off2] = total
            waits2[f, off2] = send(
                part.at[f, off2], in2.at[f, off2 - 1], in2.at[f, off2 - 1], along[1 - f](off2)
            )
    for f in range(2):
        for off2 in (1, 3, 2):
            waits2[f, off2].wait_recv()
        zbuf[32 * f : 32 * f + 32, :] += in2[f, 0] + in2[f, 1] + in2[f, 2]
    waits = []
    for off in (4, 3, 5, 2, 6, 1, 7):
        at = pl.ds(pl.multiple_of(after(z, off, 8) * 8, 8), 8)
        waits.append(send(zbuf.at[at], zin.at[off - 1], zin.at[off - 1], along_z(off)))

    first = 512 * q + (1 - zh) * (128 * x + 32 * y) + zh * (128 * y + 32 * x) + 8 * zl
    chosen = (iota((8, 1024), 1) == iota((8, 1024), 0) + first).astype(BF16)
    mine = dot(chosen, nmat[...].astype(BF16), 1, 1)
    k_of = [mine[:, d : d + 1] * (2.0 * math.pi / LENGTHS[d]) for d in range(3)]
    norm = k_of[0] * k_of[0] + k_of[1] * k_of[1] + k_of[2] * k_of[2]
    inside = lax.div(first, WAVES)
    source = pl.multiple_of(first - inside * WAVES, 8)
    weight = amp[...] * gain[pl.ds(source, 8), :] * jnp.exp(-width[...] * norm)
    weight = jnp.where(rows8 + first < WAVES, weight * (1.0 / VOLUME), 0.0)

    rows128 = iota((128, 128), 0)

    def mark(g, carry):
        for s in range(4):
            lane = lax.bitwise_and(nbr[0, 0, pl.ds(g * 4 + s, 1), :], 127)
            marks[g, :, 128 * s : 128 * s + 128] = (rows128 == lane).astype(F32).astype(BF16)
        return carry

    lax.fori_loop(0, 16, mark, 0)
    for d in range(8):
        gmarks[:, 128 * d : 128 * d + 128] = (
            (rows128 == gidx[0, 0, d : d + 1, :]).astype(F32).astype(BF16)
        )

    for w in waits:
        w.wait_recv()
    total = zbuf[pl.ds(pl.multiple_of(z * 8, 8), 8), :]
    for i in range(7):
        total = total + zin[i]
    result = weight * total
    mine_z = pl.ds(pl.multiple_of(z * 8, 8), 8)
    c3[mine_z, :] = result
    waits = []
    for off in (4, 3, 5, 2, 6, 1, 7):
        at = pl.ds(pl.multiple_of(before(z, off, 8) * 8, 8), 8)
        waits.append(send(c3.at[mine_z], c3.at[mine_z], c3.at[at], along_z(off)))

    power = result * total
    strain = jnp.sum(width[...] * power, axis=1, keepdims=True)
    energy = 0.5 * jnp.sum(jnp.sum(power, axis=1, keepdims=True), axis=0, keepdims=True)
    lanes8 = iota((8, 128), 1)
    tile = jnp.where((rows8 == lanes8) & (rows8 < 3), energy, 0.0)
    for a in range(3):
        for b in range(a, 3):
            s = jnp.sum(k_of[a] * k_of[b] * strain, axis=0, keepdims=True)
            there = (rows8 == a) & (lanes8 == b)
            if a != b:
                there = there | ((rows8 == b) & (lanes8 == a))
            tile = tile - jnp.where(there, s, 0.0)

    fgrad[...] = jnp.zeros((256, 128), F32)
    cgrad[...] = jnp.zeros((16, 256), F32)

    for w in waits:
        w.wait_recv()

    rounds = (1, 3, 2)
    waits2, waits1 = {}, {}

    def spread(f, off2, piece, src):
        for off in (2, 1, 3):
            waits1[f, off, off2] = send(
                src,
                coef.at[f, place[f], piece],
                coef.at[f, before(place[f], off, 4), piece],
                along[f](off),
            )

    for off2 in (2, 1, 3):
        for f in range(2):
            waits2[f, off2] = send(
                c3.at[32 * f : 32 * f + 32],
                coef.at[f, place[f], second[f]],
                coef.at[f, place[f], before(second[f], off2, 4)],
                along[1 - f](off2),
            )
    for f in range(2):
        spread(f, 0, second[f], c3.at[32 * f : 32 * f + 32])
        coef[f, place[f], second[f]] = c3[32 * f : 32 * f + 32, :]
    for off2 in rounds:
        for f in range(2):
            waits2[f, off2].wait_recv()
            piece = before(second[f], off2, 4)
            spread(f, off2, piece, coef.at[f, place[f], piece])

    def back(f, chunk, low, high):
        c = coef[f, chunk].reshape(128, 128)
        hi, lo = halves(c)
        fgrad[low:high, :] += dot(
            tturn[f, chunk, low:high, :], jnp.concatenate([hi, hi, lo], axis=0), 1, 0
        )
        a = dot(jnp.concatenate([hi, lo, hi], axis=1), uturn[:, low:high], 1, 0)
        turned = a * tab[1 - f, chunk, :, low:high]
        if f == 0:
            turned = -turned
        hi, lo = halves(turned)
        n = nmat[:, pl.ds(pl.multiple_of(q * 512 + chunk * 128, 128), 128)].astype(BF16)
        cgrad[:, low:high] += dot(
            jnp.concatenate([n, n], axis=1), jnp.concatenate([hi, lo], axis=0), 1, 0
        )

    for f in range(2):
        back(f, place[f], 0, 256)
    for off in rounds:
        for f in range(2):
            for off2 in (0, 1, 3, 2):
                waits1[f, off, off2].wait_recv()
            chunk = before(place[f], off, 4)
            if off == 2 and f == 1:
                back(f, chunk, 128, 256)
                xout[0:128, :] = fgrad[128:256, :]
                xout[128:144, :] = cgrad[:, 128:256]
                wait_mate = send(xout, xin, xin, partner)
                back(f, chunk, 0, 128)
            else:
                back(f, chunk, 0, 256)
    fown = fgrad[0:128, :] + gshort[...]
    wait_mate.wait_recv()

    du = (fown + xin[0:128, :]) * dsilu[...]
    daggregate = dot(du, wmix[...], 1, 1, HIGH)
    basis[...] = dot(w2[...], daggregate, 1, 1, HIGH)

    def radial_back(r, carry):
        rate, grad = carry
        d = basis[pl.ds(pl.multiple_of(r * 8, 8), 8), :] * (-2.0 * rate)
        k = kinds[...]
        chosen = jnp.zeros((SLOTS, 128), F32)
        for s in range(SPECIES):
            chosen = jnp.where(k == s, d[s : s + 1, :], chosen)
        return rate * GROWTH, grad + chosen * expo[r]

    _, slope = lax.fori_loop(
        0, BASIS, radial_back, (jnp.float32(RATE), jnp.zeros((SLOTS, 128), F32))
    )
    spent = []
    for d in range(3):
        g = slope * vec[d]
        vgrad[d] = g
        spent.append(jnp.sum(g, axis=0, keepdims=True))
    for a in range(3):
        for b in range(a, 3):
            s = jnp.sum(vgrad[a] * vec[b], axis=0, keepdims=True)
            s = jnp.sum(s, axis=1, keepdims=True)
            there = (rows8 == a) & (lanes8 == b)
            if a != b:
                there = there | ((rows8 == b) & (lanes8 == a))
            tile = tile - jnp.where(there, s, 0.0)

    def gather(buffer, value, me, to):
        buffer[me] = value
        return [
            send(buffer.at[me], buffer.at[me], buffer.at[before(me, off, 16)], to(off))
            for off in (8, 7, 9, 6, 10, 5, 11, 4, 12, 3, 13, 2, 14, 1, 15)
        ]

    def add_up(buffer):
        value = buffer[0]
        for i in range(1, 16):
            value = value + buffer[i]
        return value

    waits_v = gather(va, tile, m_zq, among_zq)

    rows16 = iota((16, 128), 0)

    def scatter(g, total):
        left = []
        for s in range(4):
            at = pl.ds(g * 4 + s, 1)
            page = lax.shift_right_logical(nbr[0, 0, at, :], 7)
            lines = jnp.concatenate(
                [jnp.where(rows16 == page, vgrad[d, at, :], 0.0) for d in range(3)], axis=0
            )
            left.append(jnp.concatenate(halves(lines), axis=0))
        return total + dot(jnp.concatenate(left, axis=1), marks[g], 1, 1)

    total = lax.fori_loop(0, SLOTS // 4, scatter, jnp.zeros((96, 128), F32))
    tgrad[...] = total[0:48, :] + total[48:96, :]
    for p in range(8):
        for d in range(3):
            gback[p, d : d + 1, :] = tgrad[16 * d + p + 1 : 16 * d + p + 2, :]
    waits_g = [send(gback.at[p], gret.at[7 - p], gret.at[7 - p], ghosts[p]) for p in range(8)]

    for w in waits_v:
        w.wait_recv()
    waits_v = gather(vb, add_up(va), m_xy, among_xy)
    for w in waits_g:
        w.wait_recv()
    left = []
    for d in range(8):
        hi, lo = halves(jnp.concatenate([gret[d], jnp.zeros((8, 128), F32)], axis=0))
        left.append(jnp.concatenate([hi, lo], axis=0))
    back_home = dot(jnp.concatenate(left, axis=1), gmarks[...], 1, 1)
    back_home = back_home[0:16, :] + back_home[16:32, :]
    moved = cgrad[:, 0:128] + xin[128:144, :]
    for d in range(3):
        grad = (
            tgrad[16 * d : 16 * d + 1, :]
            - spent[d]
            + moved[d : d + 1, :] * (2.0 * math.pi / LENGTHS[d])
            + back_home[d : d + 1, :]
        )
        out[d : d + 1, :] = -grad
    for w in waits_v:
        w.wait_recv()
    out[4:7, :] = (add_up(vb) * (1.0 / VOLUME))[0:3, :]
    for copy in started:
        copy.wait_send()


def per_device(
    positions, species, counts, neighbours, ghost_index, wave_numbers, embedding,
    w_radial, w_mix, w_read, w_out, amplitude, kernel_width, filter_gain,
):
    result = pl.pallas_call(
        kernel,
        out_shape=jax.ShapeDtypeStruct((8, 128), F32),
        in_specs=[pl.BlockSpec(memory_space=pltpu.HBM)] * 14,
        out_specs=pl.BlockSpec(memory_space=pltpu.VMEM),
        scratch_shapes=[pltpu.VMEM(shape, dtype) for shape, dtype in INPUTS]
        + [pltpu.VMEM(shape, dtype) for _, shape, dtype in SCRATCH]
        + [
            pltpu.SemaphoreType.DMA((N_COPIES,)),
            pltpu.SemaphoreType.DMA((N_COPIES,)),
            pltpu.SemaphoreType.DMA((14,)),
        ],
        compiler_params=pltpu.CompilerParams(collective_id=0, has_side_effects=True),
        name="ewald",
    )(
        positions, species, counts, neighbours, ghost_index, wave_numbers, embedding,
        w_radial, w_mix, w_read, w_out.reshape(1, 128), amplitude.reshape(1, 128),
        kernel_width.reshape(1, 128), filter_gain,
    )
    return result[0:3].reshape(3, 1, 1, 128), result[4:7, 0:3]


def solution(mesh):
    return jax.shard_map(
        per_device,
        mesh=mesh,
        in_specs=(
            P(None, "row", "col", None),
            P("row", "col", None),
            P("row", "col", None),
            P("row", "col", None, None),
            P("row", "col", None, None),
            P(), P(), P(), P(), P(), P(), P(), P(), P(),
        ),
        out_specs=(P(None, "row", "col", None), P()),
        check_vma=False,
    )
```

time: 71.6 us -> 64.1 us (0.90)
  Pallas kernels: 69 us -> 61.4 us
    pallas_call x1, Pallas kernels: 69 us -> 61.4 us  [per_device(): pl.pallas_call(kernel, out_shape=jax.ShapeDtypeStruct((8, 128), F32), in_...]
    unnamed x6 -> x3, local copies, waits for them, and re-layouts: 1.76 us -> 0.57 us
    reshape x0 -> x1, local copies, waits for them, and re-layouts: none -> 0.74 us  [per_device(): return (result[0:3].reshape(3, 1, 1, 128), result[4:7, 0:3])]
where the time goes in v2:
time: 64.1 us; the launch traced here: 63.9 us
  Pallas kernels  61.4 us (96%)
  local copies, waits for them, and re-layouts  1.89 us (3%)
  between operations  0.65 us (1%)
    pallas_call x1, Pallas kernels, per_device(): pl.pallas_call(kernel, out_shape=jax.ShapeDtypeStruct((8, 128), F32), in_...  61.4 us

profile of v2, /device:TPU:1, one launch (start us, length us, event | category | flops | bytes accessed | tf_op | source)
XLA Modules:
  0.0 63.9 jit_solution(17488469144735045997)
XLA Ops:
  0.6 61.4 %ewald.1 = f32[8,128]{1,0:T(8,128)} custom-call(f32[3,1,1,128]{3,2,1,0:T(1,128)} %refs_0_.1, s32[1,1,128]{2,1,0:T(1,128)} %refs_1_.1, s32[1,1,128]{2,1,0:T(1,128)} %refs_2_.1, s32[1,1,64,128]{3,2,1,0:T(8,128)} %refs_3_.1, s32[1,1,8,128]{3,2,1,0:T(8,128)} %refs_4_.1, s32[3,1000]{1,0:T(4,128)} %refs_5_.1, f32[6,128]{1,0:T(8,128)} %refs_6_.1, ...), custom_call_target="tpu_custom_call" | custom-call | tf_op jit(solution)/shard_map/ewald/pallas_call | solution.py:590
  62.0 0.0 copy-start
  62.1 0.7 %slice_bitcast_fusion = f32[3,1,1,128]{3,0,2,1:T(4,128)S(1)} fusion(f32[8,128]{1,0:T(8,128)} %ewald.1), kind=kLoop, calls=%fused_computation | loop fusion | bytes 3072 | tf_op jit(solution)/shard_map/reshape | solution.py:609
  62.8 0.6 copy.16
  63.4 0.0 copy-done
  63.4 0.6 slice.7
Async XLA Ops:
  62.0 1.3 %copy-start = (f32[8,128]{1,0:T(8,128)S(1)}, f32[8,128]{1,0:T(8,128)}, u32[]{:S(2)}) copy-start(f32[8,128]{1,0:T(8,128)} %ewald.1) | copy-start | bytes 12292

commit v3 on v2

--- a/solution.py
+++ b/solution.py
@@ -67,7 +67,9 @@
     return lax.broadcasted_iota(jnp.int32, shape, dim)
 
 
-N_COPIES = 130
+N_COPIES = 132
+FAR_FIRST = (8, 7, 9, 6, 10, 5, 11, 4, 12, 3, 13, 2, 14, 1, 15)
+PAIRS = ((0, 0), (0, 1), (0, 2), (1, 1), (1, 2), (2, 2))
 INPUTS = (
     ((3, 1, 1, 128), F32), ((1, 1, 128), jnp.int32), ((1, 1, 128), jnp.int32),
     ((1, 1, 64, 128), jnp.int32), ((1, 1, 8, 128), jnp.int32), ((3, 1000), jnp.int32),
@@ -91,6 +93,8 @@
     ("xout", (144, 128), F32), ("xin", (144, 128), F32),
     ("marks", (16, 128, 512), BF16), ("gmarks", (128, 1024), BF16),
     ("vgrad", (3, 64, 128), F32), ("tgrad", (48, 128), F32),
+    ("pair", (6, 64, 128), F32), ("moment", (6, 128, 128), F32),
+    ("uvir", (2, 6, 128, 128), F32),
     ("va", (16, 8, 128), F32), ("vb", (16, 8, 128), F32),
 )
 
@@ -105,7 +109,7 @@
         own, mate, gsend, pages, gback, gret, nmat, umat, tab, tsplit, tturn, emb8, w2,
         vec, kinds, dist, expo, basis, upd, usplit, uturn, dsilu, gshort,
         sums, in1, part, in2, zin, zbuf, c3, coef, fgrad, cgrad, xout, xin,
-        marks, gmarks, vgrad, tgrad, va, vb,
+        marks, gmarks, vgrad, tgrad, pair, moment, uvir, va, vb,
     ) = named
     row = lax.axis_index("row")
     col = lax.axis_index("col")
@@ -150,17 +154,17 @@
     def after(i, off, n):
         return lax.rem(i + off, n)
 
+    loads = [pltpu.make_async_copy(ins[i], here[i], lsem.at[i]) for i in range(14)]
+    for copy in loads:
+        copy.start()
     barrier = pltpu.get_barrier_semaphore()
     greeted = (
         ghosts
-        + [among_zq(off) for off in range(1, 16)]
-        + [among_xy(off) for off in range(1, 16)]
+        + [among_zq(off) for off in FAR_FIRST]
+        + [among_xy(off) for off in FAR_FIRST]
     )
     for who in greeted:
         pl.semaphore_signal(barrier, inc=1, device_id=who, device_id_type=MESH)
-    loads = [pltpu.make_async_copy(ins[i], here[i], lsem.at[i]) for i in range(14)]
-    for copy in loads:
-        copy.start()
 
     started = []
 
@@ -287,7 +291,7 @@
         kinds[pl.ds(at, 8), :] = jnp.where(rows8 + at < live, picked[3], -1.0)
         return carry
 
-    lax.fori_loop(0, 8, edge, 0)
+    lax.fori_loop(0, 8, edge, 0, unroll=2)
 
     def radial(r, rate):
         e = jnp.exp(dist[...] * (-rate))
@@ -300,7 +304,7 @@
         basis[pl.ds(pl.multiple_of(r * 8, 8), 8), :] = tile
         return rate * GROWTH
 
-    lax.fori_loop(0, BASIS, radial, jnp.float32(RATE))
+    lax.fori_loop(0, BASIS, radial, jnp.float32(RATE), unroll=4)
 
     aggregate = dot(basis[...], w2[...], 0, 0, HIGH)
     u = dot(aggregate, wmix[...], 1, 0, HIGH)
@@ -318,7 +322,9 @@
         hi, lo = halves(value)
         for p, half in enumerate((hi, hi, lo)):
             usplit[384 * side + 128 * p : 384 * side + 128 * p + 128, :] = half
-        hi, lo = halves(value.T)
+
+    def split_turned(side):
+        hi, lo = halves(upd[128 * side : 128 * side + 128, :].T)
         for p, half in enumerate((hi, hi, lo)):
             uturn[128 * p : 128 * p + 128, 128 * side : 128 * side + 128] = half
 
@@ -396,6 +402,26 @@
             (rows128 == gidx[0, 0, d : d + 1, :]).astype(F32).astype(BF16)
         )
 
+    split_turned(0)
+    split_turned(1)
+    for m, (a, b) in enumerate(PAIRS):
+        pair[m] = vec[a] * vec[b]
+
+    def moments(r, rate):
+        e = expo[r] * (2.0 * rate)
+        k = kinds[...]
+        parts = [jnp.where(k == s, e, 0.0) for s in range(SPECIES)]
+        for m in range(6):
+            v = pair[m]
+            tile = jnp.zeros((8, 128), F32)
+            for s in range(SPECIES):
+                total = jnp.sum(parts[s] * v, axis=0, keepdims=True)
+                tile = jnp.where(rows8 == s, total, tile)
+            moment[m, pl.ds(pl.multiple_of(r * 8, 8), 8), :] = tile
+        return rate * GROWTH
+
+    lax.fori_loop(0, BASIS, moments, jnp.float32(RATE))
+
     for w in waits:
         w.wait_recv()
     total = zbuf[pl.ds(pl.multiple_of(z * 8, 8), 8), :]
@@ -422,6 +448,10 @@
                 there = there | ((rows8 == b) & (lanes8 == a))
             tile = tile - jnp.where(there, s, 0.0)
 
+    for m in range(6):
+        answer = dot(moment[m], w2[...], 0, 0, HIGH)
+        uvir[0, m] = dot(answer, wmix[...], 1, 0, HIGH) * dsilu[...]
+    wait_uvir = send(uvir.at[0], uvir.at[1], uvir.at[1], partner)
     fgrad[...] = jnp.zeros((256, 128), F32)
     cgrad[...] = jnp.zeros((16, 256), F32)
 
@@ -488,7 +518,29 @@
                 back(f, chunk, 0, 128)
             else:
                 back(f, chunk, 0, 256)
+    def gather(buffer, value, me, to):
+        buffer[me] = value
+        return [
+            send(buffer.at[me], buffer.at[me], buffer.at[before(me, off, 16)], to(off))
+            for off in FAR_FIRST
+        ]
+
+    def add_up(buffer):
+        value = buffer[0]
+        for i in range(1, 16):
+            value = value + buffer[i]
+        return value
+
     fown = fgrad[0:128, :] + gshort[...]
+    wait_uvir.wait_recv()
+    for m, (a, b) in enumerate(PAIRS):
+        s = jnp.sum(fown * uvir[0, m] + fgrad[128:256, :] * uvir[1, m], axis=0, keepdims=True)
+        s = jnp.sum(s, axis=1, keepdims=True)
+        there = (rows8 == a) & (lanes8 == b)
+        if a != b:
+            there = there | ((rows8 == b) & (lanes8 == a))
+        tile = tile + jnp.where(there, s, 0.0)
+    waits_v = gather(va, tile, m_zq, among_zq)
     wait_mate.wait_recv()
 
     du = (fown + xin[0:128, :]) * dsilu[...]
@@ -505,36 +557,13 @@
         return rate * GROWTH, grad + chosen * expo[r]
 
     _, slope = lax.fori_loop(
-        0, BASIS, radial_back, (jnp.float32(RATE), jnp.zeros((SLOTS, 128), F32))
+        0, BASIS, radial_back, (jnp.float32(RATE), jnp.zeros((SLOTS, 128), F32)), unroll=4
     )
     spent = []
     for d in range(3):
         g = slope * vec[d]
         vgrad[d] = g
         spent.append(jnp.sum(g, axis=0, keepdims=True))
-    for a in range(3):
-        for b in range(a, 3):
-            s = jnp.sum(vgrad[a] * vec[b], axis=0, keepdims=True)
-            s = jnp.sum(s, axis=1, keepdims=True)
-            there = (rows8 == a) & (lanes8 == b)
-            if a != b:
-                there = there | ((rows8 == b) & (lanes8 == a))
-            tile = tile - jnp.where(there, s, 0.0)
-
-    def gather(buffer, value, me, to):
-        buffer[me] = value
-        return [
-            send(buffer.at[me], buffer.at[me], buffer.at[before(me, off, 16)], to(off))
-            for off in (8, 7, 9, 6, 10, 5, 11, 4, 12, 3, 13, 2, 14, 1, 15)
-        ]
-
-    def add_up(buffer):
-        value = buffer[0]
-        for i in range(1, 16):
-            value = value + buffer[i]
-        return value
-
-    waits_v = gather(va, tile, m_zq, among_zq)
 
     rows16 = iota((16, 128), 0)
 
@@ -549,7 +578,7 @@
             left.append(jnp.concatenate(halves(lines), axis=0))
         return total + dot(jnp.concatenate(left, axis=1), marks[g], 1, 1)
 
-    total = lax.fori_loop(0, SLOTS // 4, scatter, jnp.zeros((96, 128), F32))
+    total = lax.fori_loop(0, SLOTS // 4, scatter, jnp.zeros((96, 128), F32), unroll=2)
     tgrad[...] = total[0:48, :] + total[48:96, :]
     for p in range(8):
         for d in range(3):
@@ -583,6 +612,12 @@
         copy.wait_send()
 
 
+def hand_over(result, force, virial):
+    for d in range(3):
+        force[d, 0] = result[d : d + 1, :]
+    virial[...] = result[4:7, 0:3]
+
+
 def per_device(
     positions, species, counts, neighbours, ghost_index, wave_numbers, embedding,
     w_radial, w_mix, w_read, w_out, amplitude, kernel_width, filter_gain,
@@ -606,7 +641,19 @@
         w_radial, w_mix, w_read, w_out.reshape(1, 128), amplitude.reshape(1, 128),
         kernel_width.reshape(1, 128), filter_gain,
     )
-    return result[0:3].reshape(3, 1, 1, 128), result[4:7, 0:3]
+    return pl.pallas_call(
+        hand_over,
+        out_shape=(
+            jax.ShapeDtypeStruct((3, 1, 1, 128), F32),
+            jax.ShapeDtypeStruct((3, 3), F32),
+        ),
+        in_specs=[pl.BlockSpec(memory_space=pltpu.VMEM)],
+        out_specs=(
+            pl.BlockSpec(memory_space=pltpu.VMEM),
+            pl.BlockSpec(memory_space=pltpu.VMEM),
+        ),
+        name="hand_over",
+    )(result)
 
 
 def solution(mesh):

time: 64.1 us -> 61.9 us (0.966)
  local copies, waits for them, and re-layouts: 1.89 us -> 0 us
    pallas_call x1, Pallas kernels: 61.4 us -> 59.8 us  [per_device(): pl.pallas_call(kernel, out_shape=jax.ShapeDtypeStruct((8, 128), F32), in_...]
    pallas_call x0 -> x1, Pallas kernels: none -> 1.27 us  [per_device(): pl.pallas_call(hand_over, out_shape=(jax.ShapeDtypeStruct((3, 1, 1, 128),...]
    reshape x1 -> x0, local copies, waits for them, and re-layouts: 0.74 us -> none  [per_device(): return (result[0:3].reshape(3, 1, 1, 128), result[4:7, 0:3])]
where the time goes in v3:
time: 61.9 us; the launch traced here: 61.7 us
  Pallas kernels  61.1 us (99%)
  between operations  0.64 us (1%)
    pallas_call x1, Pallas kernels, per_device(): pl.pallas_call(kernel, out_shape=jax.ShapeDtypeStruct((8, 128), F32), in_...  59.8 us
    pallas_call x1, Pallas kernels, per_device(): pl.pallas_call(hand_over, out_shape=(jax.ShapeDtypeStruct((3, 1, 1, 128),...  1.27 us

profile of v3, /device:TPU:1, one launch (start us, length us, event | category | flops | bytes accessed | tf_op | source)
XLA Modules:
  0.0 61.7 jit_solution(5595784274695981222)
XLA Ops:
  0.6 59.8 %ewald.1.result = f32[8,128]{1,0:T(8,128)} custom-call(f32[3,1,1,128]{3,2,1,0:T(1,128)} %refs_0_.1, s32[1,1,128]{2,1,0:T(1,128)} %refs_1_.1, s32[1,1,128]{2,1,0:T(1,128)} %refs_2_.1, s32[1,1,64,128]{3,2,1,0:T(8,128)} %refs_3_.1, s32[1,1,8,128]{3,2,1,0:T(8,128)} %refs_4_.1, s32[3,1000]{1,0:T(4,128)} %refs_5_.1, f32[6,128]{1,0:T(8,128)} %refs_6_.1, ...), custom_call_target="tpu_custom_call" | custom-call | tf_op jit(solution)/shard_map/ewald/pallas_call | solution.py:625
  60.5 1.3 %hand_over.1 = (f32[3,1,1,128]{3,2,1,0:T(1,128)}, f32[3,3]{1,0:T(4,128)}) custom-call(f32[8,128]{1,0:T(8,128)} %ewald.1.result), custom_call_target="tpu_custom_call" | custom-call | tf_op jit(solution)/shard_map/hand_over/pallas_call | solution.py:644

commit v4 on v3

--- a/solution.py
+++ b/solution.py
@@ -68,7 +68,8 @@
 
 
 N_COPIES = 132
-FAR_FIRST = (8, 7, 9, 6, 10, 5, 11, 4, 12, 3, 13, 2, 14, 1, 15)
+FAR_ZQ = (9, 8, 7, 6, 11, 10, 5, 4, 13, 12, 3, 2, 15, 14, 1)
+FAR_XY = (10, 9, 11, 6, 14, 5, 7, 13, 15, 8, 2, 4, 12, 1, 3)
 PAIRS = ((0, 0), (0, 1), (0, 2), (1, 1), (1, 2), (2, 2))
 INPUTS = (
     ((3, 1, 1, 128), F32), ((1, 1, 128), jnp.int32), ((1, 1, 128), jnp.int32),
@@ -79,8 +80,9 @@
 SCRATCH = (
     ("own", (8, 128), F32), ("mate", (8, 128), F32), ("gsend", (8, 8, 128), F32),
     ("pages", (9, 8, 128), F32), ("gback", (8, 8, 128), F32), ("gret", (8, 8, 128), F32),
-    ("nmat", (16, 1024), F32), ("umat", (16, 256), F32), ("tab", (2, 4, 128, 256), F32),
-    ("tsplit", (2, 4, 128, 768), BF16), ("tturn", (2, 4, 256, 384), BF16),
+    ("nmat", (16, 1024), F32), ("umat", (16, 256), F32), ("tab", (2, 4, 4, 32, 256), F32),
+    ("tsplit", (2, 4, 128, 768), BF16), ("thi", (2, 4, 4, 32, 256), BF16),
+    ("tlo", (2, 4, 4, 32, 256), BF16), ("nb", (3, 4, 4, 32, 128), F32),
     ("emb8", (8, 128), F32), ("w2", (128, 128), F32),
     ("vec", (3, 64, 128), F32), ("kinds", (64, 128), F32), ("dist", (64, 128), F32),
     ("expo", (16, 64, 128), F32), ("basis", (128, 128), F32), ("upd", (256, 128), F32),
@@ -89,13 +91,13 @@
     ("sums", (2, 4, 4, 32, 128), F32), ("in1", (2, 3, 4, 32, 128), F32),
     ("part", (2, 4, 32, 128), F32), ("in2", (2, 3, 32, 128), F32),
     ("zin", (7, 8, 128), F32), ("zbuf", (64, 128), F32), ("c3", (64, 128), F32),
-    ("coef", (2, 4, 4, 32, 128), F32), ("fgrad", (256, 128), F32), ("cgrad", (16, 256), F32),
-    ("xout", (144, 128), F32), ("xin", (144, 128), F32),
+    ("coef", (2, 4, 4, 32, 128), F32), ("fgrad", (128, 256), F32), ("cgrad", (3, 8, 256), F32),
+    ("xout", (152, 128), F32), ("xin", (152, 128), F32),
     ("marks", (16, 128, 512), BF16), ("gmarks", (128, 1024), BF16),
     ("vgrad", (3, 64, 128), F32), ("tgrad", (48, 128), F32),
     ("pair", (6, 64, 128), F32), ("moment", (6, 128, 128), F32),
     ("uvir", (2, 6, 128, 128), F32),
-    ("va", (16, 8, 128), F32), ("vb", (16, 8, 128), F32),
+    ("va", (16, 1, 128), F32), ("vb", (16, 1, 128), F32),
 )
 
 
@@ -106,7 +108,7 @@
     ssem, rsem, lsem = refs[29 + len(SCRATCH) :]
     (pos, spec, cnt, nbr, gidx, wn, emb, wrad, wmix, wread, wout, amp, width, gain) = here
     (
-        own, mate, gsend, pages, gback, gret, nmat, umat, tab, tsplit, tturn, emb8, w2,
+        own, mate, gsend, pages, gback, gret, nmat, umat, tab, tsplit, thi, tlo, nb, emb8, w2,
         vec, kinds, dist, expo, basis, upd, usplit, uturn, dsilu, gshort,
         sums, in1, part, in2, zin, zbuf, c3, coef, fgrad, cgrad, xout, xin,
         marks, gmarks, vgrad, tgrad, pair, moment, uvir, va, vb,
@@ -120,48 +122,55 @@
     zh = lax.div(col, 4)
     z = zh * 4 + zl
 
-    def device(q, x, y, z):
-        return (y * 8 + lax.rem(z, 4) * 2 + q, lax.div(z, 4) * 4 + x)
-
-    ghosts = [
-        (lax.rem(row + a + ROWS, ROWS), lax.rem(col + b + COLS, COLS)) for a, b in DIRECTIONS
-    ]
-    partner = device(1 - q, x, y, z)
+    xs = [x] + [lax.rem(x + off, 4) for off in (1, 2, 3)]
+    ys = [y] + [lax.rem(y + off, 4) for off in (1, 2, 3)]
+    zs = [z] + [lax.rem(z + off, 8) for off in range(1, 8)]
+    z_cols = [lax.div(at, 4) * 4 for at in zs]
+    z_rows = [(at - high) * 2 for at, high in zip(zs, z_cols)]
+    y_rows = [at * 8 for at in ys]
+    cores = [q, 1 - q]
+    x_base = z_cols[0]
+    y_base = z_rows[0] + q
+
+    up, down = lax.rem(row + 1, ROWS), lax.rem(row + ROWS - 1, ROWS)
+    east, west = lax.rem(col + 1, COLS), lax.rem(col + COLS - 1, COLS)
+    ghosts = [((down, row, up)[a + 1], (west, col, east)[b + 1]) for a, b in DIRECTIONS]
+    partner = (row + 1 - 2 * q, col)
 
     def along_x(off):
-        return device(q, lax.rem(x + off, 4), y, z)
+        return (row, x_base + xs[off])
 
     def along_y(off):
-        return device(q, x, lax.rem(y + off, 4), z)
+        return (y_rows[off] + y_base, col)
 
     def along_z(off):
-        return device(q, x, y, lax.rem(z + off, 8))
+        return (y_rows[0] + z_rows[off] + q, z_cols[off] + x)
+
+    def among_zq(off):
+        dz, dq = off // 2, off % 2
+        return (y_rows[0] + z_rows[dz] + cores[dq], z_cols[dz] + x)
+
+    def among_xy(off):
+        dx, dy = off // 4, off % 4
+        return (y_rows[dy] + y_base, x_base + xs[dx])
 
     m_zq = z * 2 + q
     m_xy = x * 4 + y
 
-    def among_zq(off):
-        m = lax.rem(m_zq + off, 16)
-        return device(lax.rem(m, 2), x, y, lax.div(m, 2))
-
-    def among_xy(off):
-        m = lax.rem(m_xy + off, 16)
-        return device(q, lax.div(m, 4), lax.rem(m, 4), z)
-
-    def before(i, off, n):
-        return lax.rem(i + n - off, n)
-
-    def after(i, off, n):
-        return lax.rem(i + off, n)
+    def from_zq(off):
+        dz, dq = off // 2, off % 2
+        return zs[(8 - dz) % 8] * 2 + cores[dq]
+
+    def from_xy(off):
+        dx, dy = off // 4, off % 4
+        return xs[(4 - dx) % 4] * 4 + ys[(4 - dy) % 4]
 
     loads = [pltpu.make_async_copy(ins[i], here[i], lsem.at[i]) for i in range(14)]
     for copy in loads:
         copy.start()
     barrier = pltpu.get_barrier_semaphore()
     greeted = (
-        ghosts
-        + [among_zq(off) for off in FAR_FIRST]
-        + [among_xy(off) for off in FAR_FIRST]
+        ghosts + [among_zq(off) for off in FAR_ZQ] + [among_xy(off) for off in FAR_XY]
     )
     for who in greeted:
         pl.semaphore_signal(barrier, inc=1, device_id=who, device_id_type=MESH)
@@ -243,20 +252,19 @@
         turns = turns - jnp.floor(turns + 0.5)
         w = turns * turns
         for f, value in enumerate((horner(COSINE, w), horner(SINE, w) * turns)):
-            tab[f, i] = value
+            tab[f, i] = value.reshape(4, 32, 256)
             hi, lo = halves(value)
+            thi[f, i] = hi.reshape(4, 32, 256)
+            tlo[f, i] = lo.reshape(4, 32, 256)
             for side in range(2):
                 mine = slice(128 * side, 128 * side + 128)
                 for p, half in enumerate((hi, lo, hi)):
                     at = 384 * side + 128 * p
                     tsplit[f, i, :, at : at + 128] = half[:, mine]
-        turns = dot(fractions, block, 0, 0)
-        turns = turns - jnp.floor(turns + 0.5)
-        w = turns * turns
-        for f, value in enumerate((horner(COSINE, w), horner(SINE, w) * turns)):
-            hi, lo = halves(value)
-            for p, half in enumerate((hi, lo, hi)):
-                tturn[f, i, :, 128 * p : 128 * p + 128] = half
+        for d in range(3):
+            nb[d, i] = dot(block, (iota((16, 128), 0) == d).astype(F32).astype(BF16), 0, 0).reshape(
+                4, 32, 128
+            )
         return carry
 
     lax.fori_loop(0, 4, trig, 0)
@@ -312,10 +320,10 @@
     mine = start + u * gate
     upd[0:128, :] = mine
     wait_mate = send(upd.at[0:128], upd.at[128:256], upd.at[128:256], partner)
-    dsilu[...] = gate * (1.0 + u * (1.0 - gate))
+    dsilu[...] = (gate * (1.0 + u * (1.0 - gate))).T
     p = dot(mine, wread[...], 1, 0, HIGH)
     gate = 1.0 / (1.0 + jnp.exp(-p))
-    gshort[...] = dot(wout[...] * (gate * (1.0 + p * (1.0 - gate))), wread[...], 1, 1, HIGH)
+    gshort[...] = dot(wread[...], wout[...] * (gate * (1.0 + p * (1.0 - gate))), 1, 1, HIGH)
 
     def split(side):
         value = upd[128 * side : 128 * side + 128, :]
@@ -332,21 +340,23 @@
     wait_mate.wait_recv()
     split(1)
 
-    place = (x, y)
-    second = (y, x)
+    places = (xs, ys)
+    seconds = (ys, xs)
     along = (along_x, along_y)
     order = (2, 1, 3, 0)
     waits1 = {}
     for off in order:
+        chunks = [places[f][off] for f in range(2)]
+        lines = jnp.concatenate([tsplit[f, chunks[f]] for f in range(2)], axis=0)
+        value = dot(lines, usplit[...], 1, 0).reshape(2, 4, 32, 128)
         for f in range(2):
-            chunk = after(place[f], off, 4)
-            value = dot(tsplit[f, chunk], usplit[...], 1, 0)
-            sums[f, chunk] = value.reshape(4, 32, 128)
+            chunk = chunks[f]
+            sums[f, chunk] = value[f]
             if off == 0:
                 continue
             for off2 in order:
                 waits1[f, off, off2] = send(
-                    sums.at[f, chunk, after(second[f], off2, 4)],
+                    sums.at[f, chunk, seconds[f][off2]],
                     in1.at[f, off - 1, off2],
                     in1.at[f, off - 1, off2],
                     along[f](off),
@@ -357,7 +367,7 @@
             for off in (1, 3, 2):
                 waits1[f, off, off2].wait_recv()
             total = (
-                sums[f, place[f], after(second[f], off2, 4)]
+                sums[f, places[f][0], seconds[f][off2]]
                 + in1[f, 0, off2]
                 + in1[f, 1, off2]
                 + in1[f, 2, off2]
@@ -375,7 +385,7 @@
         zbuf[32 * f : 32 * f + 32, :] += in2[f, 0] + in2[f, 1] + in2[f, 2]
     waits = []
     for off in (4, 3, 5, 2, 6, 1, 7):
-        at = pl.ds(pl.multiple_of(after(z, off, 8) * 8, 8), 8)
+        at = pl.ds(pl.multiple_of(zs[off] * 8, 8), 8)
         waits.append(send(zbuf.at[at], zin.at[off - 1], zin.at[off - 1], along_z(off)))
 
     first = 512 * q + (1 - zh) * (128 * x + 32 * y) + zh * (128 * y + 32 * x) + 8 * zl
@@ -432,28 +442,25 @@
     c3[mine_z, :] = result
     waits = []
     for off in (4, 3, 5, 2, 6, 1, 7):
-        at = pl.ds(pl.multiple_of(before(z, off, 8) * 8, 8), 8)
+        at = pl.ds(pl.multiple_of(zs[8 - off] * 8, 8), 8)
         waits.append(send(c3.at[mine_z], c3.at[mine_z], c3.at[at], along_z(off)))
 
     power = result * total
     strain = jnp.sum(width[...] * power, axis=1, keepdims=True)
     energy = 0.5 * jnp.sum(jnp.sum(power, axis=1, keepdims=True), axis=0, keepdims=True)
-    lanes8 = iota((8, 128), 1)
-    tile = jnp.where((rows8 == lanes8) & (rows8 < 3), energy, 0.0)
-    for a in range(3):
-        for b in range(a, 3):
-            s = jnp.sum(k_of[a] * k_of[b] * strain, axis=0, keepdims=True)
-            there = (rows8 == a) & (lanes8 == b)
-            if a != b:
-                there = there | ((rows8 == b) & (lanes8 == a))
-            tile = tile - jnp.where(there, s, 0.0)
-
+    lanes = iota((1, 128), 1)
+    tile = jnp.where((lanes == 0) | (lanes == 4) | (lanes == 8), energy, 0.0)
+    for a, b in PAIRS:
+        s = jnp.sum(k_of[a] * k_of[b] * strain, axis=0, keepdims=True)
+        tile = tile - jnp.where((lanes == 3 * a + b) | (lanes == 3 * b + a), s, 0.0)
+
+    turned_mix = wmix[...].T
     for m in range(6):
-        answer = dot(moment[m], w2[...], 0, 0, HIGH)
-        uvir[0, m] = dot(answer, wmix[...], 1, 0, HIGH) * dsilu[...]
+        answer = dot(w2[...], moment[m], 0, 0, HIGH)
+        uvir[0, m] = dot(turned_mix, answer, 1, 0, HIGH) * dsilu[...]
     wait_uvir = send(uvir.at[0], uvir.at[1], uvir.at[1], partner)
-    fgrad[...] = jnp.zeros((256, 128), F32)
-    cgrad[...] = jnp.zeros((16, 256), F32)
+    fgrad[...] = jnp.zeros((128, 256), F32)
+    cgrad[...] = jnp.zeros((3, 8, 256), F32)
 
     for w in waits:
         w.wait_recv()
@@ -465,8 +472,8 @@
         for off in (2, 1, 3):
             waits1[f, off, off2] = send(
                 src,
-                coef.at[f, place[f], piece],
-                coef.at[f, before(place[f], off, 4), piece],
+                coef.at[f, places[f][0], piece],
+                coef.at[f, places[f][4 - off], piece],
                 along[f](off),
             )
 
@@ -474,55 +481,54 @@
         for f in range(2):
             waits2[f, off2] = send(
                 c3.at[32 * f : 32 * f + 32],
-                coef.at[f, place[f], second[f]],
-                coef.at[f, place[f], before(second[f], off2, 4)],
+                coef.at[f, places[f][0], seconds[f][0]],
+                coef.at[f, places[f][0], seconds[f][(4 - off2) % 4]],
                 along[1 - f](off2),
             )
     for f in range(2):
-        spread(f, 0, second[f], c3.at[32 * f : 32 * f + 32])
-        coef[f, place[f], second[f]] = c3[32 * f : 32 * f + 32, :]
+        spread(f, 0, seconds[f][0], c3.at[32 * f : 32 * f + 32])
+        coef[f, places[f][0], seconds[f][0]] = c3[32 * f : 32 * f + 32, :]
     for off2 in rounds:
         for f in range(2):
             waits2[f, off2].wait_recv()
-            piece = before(second[f], off2, 4)
-            spread(f, off2, piece, coef.at[f, place[f], piece])
-
-    def back(f, chunk, low, high):
-        c = coef[f, chunk].reshape(128, 128)
+            piece = seconds[f][(4 - off2) % 4]
+            spread(f, off2, piece, coef.at[f, places[f][0], piece])
+
+    def back(f, piece):
+        c = coef[f, :, piece].reshape(128, 128)
+        hi, lo = halves(c.T)
+        t = thi[f, :, piece].reshape(128, 256)
+        fgrad[...] += dot(
+            jnp.concatenate([hi, hi, lo], axis=1),
+            jnp.concatenate([t, tlo[f, :, piece].reshape(128, 256), t], axis=0),
+            1,
+            0,
+        )
         hi, lo = halves(c)
-        fgrad[low:high, :] += dot(
-            tturn[f, chunk, low:high, :], jnp.concatenate([hi, hi, lo], axis=0), 1, 0
-        )
-        a = dot(jnp.concatenate([hi, lo, hi], axis=1), uturn[:, low:high], 1, 0)
-        turned = a * tab[1 - f, chunk, :, low:high]
+        turned = dot(jnp.concatenate([hi, lo, hi], axis=1), uturn[...], 1, 0)
+        turned = turned * tab[1 - f, :, piece].reshape(128, 256)
         if f == 0:
             turned = -turned
-        hi, lo = halves(turned)
-        n = nmat[:, pl.ds(pl.multiple_of(q * 512 + chunk * 128, 128), 128)].astype(BF16)
-        cgrad[:, low:high] += dot(
-            jnp.concatenate([n, n], axis=1), jnp.concatenate([hi, lo], axis=0), 1, 0
-        )
-
-    for f in range(2):
-        back(f, place[f], 0, 256)
-    for off in rounds:
+        for d in range(3):
+            n = nb[d, :, piece].reshape(128, 128)
+            for side in range(2):
+                mine = slice(128 * side, 128 * side + 128)
+                cgrad[d, :, mine] += jnp.sum((turned[:, mine] * n).reshape(16, 8, 128), axis=0)
+
+    for off2 in (0,) + rounds:
         for f in range(2):
-            for off2 in (0, 1, 3, 2):
+            for off in rounds:
                 waits1[f, off, off2].wait_recv()
-            chunk = before(place[f], off, 4)
-            if off == 2 and f == 1:
-                back(f, chunk, 128, 256)
-                xout[0:128, :] = fgrad[128:256, :]
-                xout[128:144, :] = cgrad[:, 128:256]
-                wait_mate = send(xout, xin, xin, partner)
-                back(f, chunk, 0, 128)
-            else:
-                back(f, chunk, 0, 256)
-    def gather(buffer, value, me, to):
+            back(f, seconds[f][(4 - off2) % 4])
+    xout[0:128, :] = fgrad[:, 128:256]
+    for d in range(3):
+        xout[128 + 8 * d : 136 + 8 * d, :] = cgrad[d, :, 128:256]
+    wait_mate = send(xout, xin, xin, partner)
+
+    def gather(buffer, value, me, to, come, offs):
         buffer[me] = value
         return [
-            send(buffer.at[me], buffer.at[me], buffer.at[before(me, off, 16)], to(off))
-            for off in FAR_FIRST
+            send(buffer.at[me], buffer.at[me], buffer.at[come(off)], to(off)) for off in offs
         ]
 
     def add_up(buffer):
@@ -531,21 +537,18 @@
             value = value + buffer[i]
         return value
 
-    fown = fgrad[0:128, :] + gshort[...]
+    fown = fgrad[:, 0:128] + gshort[...]
     wait_uvir.wait_recv()
     for m, (a, b) in enumerate(PAIRS):
-        s = jnp.sum(fown * uvir[0, m] + fgrad[128:256, :] * uvir[1, m], axis=0, keepdims=True)
+        s = jnp.sum(fown * uvir[0, m] + fgrad[:, 128:256] * uvir[1, m], axis=0, keepdims=True)
         s = jnp.sum(s, axis=1, keepdims=True)
-        there = (rows8 == a) & (lanes8 == b)
-        if a != b:
-            there = there | ((rows8 == b) & (lanes8 == a))
-        tile = tile + jnp.where(there, s, 0.0)
-    waits_v = gather(va, tile, m_zq, among_zq)
+        tile = tile + jnp.where((lanes == 3 * a + b) | (lanes == 3 * b + a), s, 0.0)
+    waits_v = gather(va, tile, m_zq, among_zq, from_zq, FAR_ZQ)
     wait_mate.wait_recv()
 
     du = (fown + xin[0:128, :]) * dsilu[...]
-    daggregate = dot(du, wmix[...], 1, 1, HIGH)
-    basis[...] = dot(w2[...], daggregate, 1, 1, HIGH)
+    daggregate = dot(wmix[...], du, 1, 0, HIGH)
+    basis[...] = dot(w2[...], daggregate, 1, 0, HIGH)
 
     def radial_back(r, carry):
         rate, grad = carry
@@ -587,7 +590,7 @@
 
     for w in waits_v:
         w.wait_recv()
-    waits_v = gather(vb, add_up(va), m_xy, among_xy)
+    waits_v = gather(vb, add_up(va), m_xy, among_xy, from_xy, FAR_XY)
     for w in waits_g:
         w.wait_recv()
     left = []
@@ -596,18 +599,23 @@
         left.append(jnp.concatenate([hi, lo], axis=0))
     back_home = dot(jnp.concatenate(left, axis=1), gmarks[...], 1, 1)
     back_home = back_home[0:16, :] + back_home[16:32, :]
-    moved = cgrad[:, 0:128] + xin[128:144, :]
+    moved = [
+        jnp.sum(
+            cgrad[d, :, 0:128] + xin[128 + 8 * d : 136 + 8 * d, :], axis=0, keepdims=True
+        )
+        for d in range(3)
+    ]
     for d in range(3):
         grad = (
             tgrad[16 * d : 16 * d + 1, :]
             - spent[d]
-            + moved[d : d + 1, :] * (2.0 * math.pi / LENGTHS[d])
+            + moved[d] * (2.0 * math.pi / LENGTHS[d])
             + back_home[d : d + 1, :]
         )
         out[d : d + 1, :] = -grad
     for w in waits_v:
         w.wait_recv()
-    out[4:7, :] = (add_up(vb) * (1.0 / VOLUME))[0:3, :]
+    out[4:5, :] = add_up(vb) * (1.0 / VOLUME)
     for copy in started:
         copy.wait_send()
 
@@ -615,7 +623,8 @@
 def hand_over(result, force, virial):
     for d in range(3):
         force[d, 0] = result[d : d + 1, :]
-    virial[...] = result[4:7, 0:3]
+    for d in range(3):
+        virial[d : d + 1, :] = result[4:5, 3 * d : 3 * d + 3]
 
 
 def per_device(
@@ -624,7 +633,7 @@
 ):
     result = pl.pallas_call(
         kernel,
-        out_shape=jax.ShapeDtypeStruct((8, 128), F32),
+        out_shape=pltpu.VMEM((8, 128), F32),
         in_specs=[pl.BlockSpec(memory_space=pltpu.HBM)] * 14,
         out_specs=pl.BlockSpec(memory_space=pltpu.VMEM),
         scratch_shapes=[pltpu.VMEM(shape, dtype) for shape, dtype in INPUTS]
@@ -653,7 +662,7 @@
             pl.BlockSpec(memory_space=pltpu.VMEM),
         ),
         name="hand_over",
-    )(result)
+    )(pltpu.with_memory_space_constraint(result, pltpu.VMEM))
 
 
 def solution(mesh):

time: 61.9 us -> 59.6 us (0.963)
  Pallas kernels: 61.1 us -> 58.9 us
    pallas_call x1, Pallas kernels: 59.8 us -> 58.2 us  [per_device(): pl.pallas_call(kernel, out_shape=pltpu.VMEM((8, 128), F32), in_specs=[pl....]
where the time goes in v4:
time: 59.6 us; the launch traced here: 59.5 us
  Pallas kernels  58.9 us (99%)
  between operations  0.64 us (1%)
    pallas_call x1, Pallas kernels, per_device(): pl.pallas_call(kernel, out_shape=pltpu.VMEM((8, 128), F32), in_specs=[pl....  58.2 us

profile of v4, /device:TPU:1, one launch (start us, length us, event | category | flops | bytes accessed | tf_op | source)
XLA Modules:
  0.0 59.5 jit_solution(12255930845620667086)
XLA Ops:
  0.6 58.2 %ewald.1.result = f32[8,128]{1,0:T(8,128)S(1)} custom-call(f32[3,1,1,128]{3,2,1,0:T(1,128)} %refs_0_.1, s32[1,1,128]{2,1,0:T(1,128)} %refs_1_.1, s32[1,1,128]{2,1,0:T(1,128)} %refs_2_.1, s32[1,1,64,128]{3,2,1,0:T(8,128)} %refs_3_.1, s32[1,1,8,128]{3,2,1,0:T(8,128)} %refs_4_.1, s32[3,1000]{1,0:T(4,128)} %refs_5_.1, f32[6,128]{1,0:T(8,128)} %refs_6_.1, ...), custom_call_target="tpu_custom_call" | custom-call | tf_op jit(solution)/shard_map/ewald/pallas_call | solution.py:634
  58.9 0.7 %hand_over.1 = (f32[3,1,1,128]{3,2,1,0:T(1,128)}, f32[3,3]{1,0:T(4,128)}) custom-call(f32[8,128]{1,0:T(8,128)S(1)} %ewald.1.result), custom_call_target="tpu_custom_call" | custom-call | tf_op jit(solution)/shard_map/hand_over/pallas_call | solution.py:653

commit v5 on v4

--- a/solution.py
+++ b/solution.py
@@ -166,8 +166,8 @@
         return xs[(4 - dx) % 4] * 4 + ys[(4 - dy) % 4]
 
     loads = [pltpu.make_async_copy(ins[i], here[i], lsem.at[i]) for i in range(14)]
-    for copy in loads:
-        copy.start()
+    for i in (0, 1, 4, 2, 3, 5, 6, 7, 8, 9, 10, 11, 12, 13):
+        loads[i].start()
     barrier = pltpu.get_barrier_semaphore()
     greeted = (
         ghosts + [among_zq(off) for off in FAR_ZQ] + [among_xy(off) for off in FAR_XY]
@@ -203,8 +203,8 @@
     umat[...] = jnp.zeros((16, 256), F32)
     emb8[...] = jnp.zeros((8, 128), F32)
     own[...] = jnp.zeros((8, 128), F32)
-    for copy in loads:
-        copy.wait()
+    for i in (0, 1, 4):
+        loads[i].wait()
 
     for d in range(3):
         own[d : d + 1, :] = pos[d, 0]
@@ -214,15 +214,17 @@
         index = jnp.broadcast_to(gidx[0, 0, d : d + 1, :], (8, 128))
         gsend[d] = jnp.take_along_axis(table, index, axis=1, mode="promise_in_bounds")
     pages[0] = table
-    numbers = wn[...].astype(F32)
-    for p in range(3):
-        nmat[3 * p : 3 * p + 3, 0:WAVES] = numbers
-
     pl.semaphore_wait(barrier, len(greeted))
     wait_mate = send(own, mate, mate, partner)
     waits = [
         send(gsend.at[d], pages.at[8 - d], pages.at[8 - d], ghosts[d]) for d in range(8)
     ]
+
+    for i in (2, 3, 5, 6, 7, 8, 9, 10, 11, 12, 13):
+        loads[i].wait()
+    numbers = wn[...].astype(F32)
+    for p in range(3):
+        nmat[3 * p : 3 * p + 3, 0:WAVES] = numbers
 
     emb8[0:SPECIES, :] = emb[...]
     kinds8 = emb8[...]
@@ -337,6 +339,11 @@
             uturn[128 * p : 128 * p + 128, 128 * side : 128 * side + 128] = half
 
     split(0)
+    for i in range(4):
+        lines = jnp.concatenate([tsplit[f, i, :, 0:384] for f in range(2)], axis=0)
+        value = dot(lines, usplit[0:384, :], 1, 0).reshape(2, 4, 32, 128)
+        for f in range(2):
+            sums[f, i] = value[f]
     wait_mate.wait_recv()
     split(1)
 
@@ -347,11 +354,11 @@
     waits1 = {}
     for off in order:
         chunks = [places[f][off] for f in range(2)]
-        lines = jnp.concatenate([tsplit[f, chunks[f]] for f in range(2)], axis=0)
-        value = dot(lines, usplit[...], 1, 0).reshape(2, 4, 32, 128)
+        lines = jnp.concatenate([tsplit[f, chunks[f], :, 384:768] for f in range(2)], axis=0)
+        value = dot(lines, usplit[384:768, :], 1, 0).reshape(2, 4, 32, 128)
         for f in range(2):
             chunk = chunks[f]
-            sums[f, chunk] = value[f]
+            sums[f, chunk] += value[f]
             if off == 0:
                 continue
             for off2 in order:
@@ -581,7 +588,7 @@
             left.append(jnp.concatenate(halves(lines), axis=0))
         return total + dot(jnp.concatenate(left, axis=1), marks[g], 1, 1)
 
-    total = lax.fori_loop(0, SLOTS // 4, scatter, jnp.zeros((96, 128), F32), unroll=2)
+    total = lax.fori_loop(0, SLOTS // 4, scatter, jnp.zeros((96, 128), F32), unroll=8)
     tgrad[...] = total[0:48, :] + total[48:96, :]
     for p in range(8):
         for d in range(3):

time: 59.6 us -> 58.7 us (0.985)
  Pallas kernels: 58.9 us -> 57.9 us
    pallas_call x1, Pallas kernels: 58.2 us -> 57.3 us  [per_device(): pl.pallas_call(kernel, out_shape=pltpu.VMEM((8, 128), F32), in_specs=[pl....]
where the time goes in v5:
time: 58.7 us; the launch traced here: 58.6 us
  Pallas kernels  57.9 us (99%)
  between operations  0.64 us (1%)
    pallas_call x1, Pallas kernels, per_device(): pl.pallas_call(kernel, out_shape=pltpu.VMEM((8, 128), F32), in_specs=[pl....  57.3 us

profile of v5, /device:TPU:1, one launch (start us, length us, event | category | flops | bytes accessed | tf_op | source)
XLA Modules:
  0.0 58.6 jit_solution(10367486364737601406)
XLA Ops:
  0.6 57.3 %ewald.1.result = f32[8,128]{1,0:T(8,128)S(1)} custom-call(f32[3,1,1,128]{3,2,1,0:T(1,128)} %refs_0_.1, s32[1,1,128]{2,1,0:T(1,128)} %refs_1_.1, s32[1,1,128]{2,1,0:T(1,128)} %refs_2_.1, s32[1,1,64,128]{3,2,1,0:T(8,128)} %refs_3_.1, s32[1,1,8,128]{3,2,1,0:T(8,128)} %refs_4_.1, s32[3,1000]{1,0:T(4,128)} %refs_5_.1, f32[6,128]{1,0:T(8,128)} %refs_6_.1, ...), custom_call_target="tpu_custom_call" | custom-call | tf_op jit(solution)/shard_map/ewald/pallas_call | solution.py:641
  57.9 0.7 %hand_over.1 = (f32[3,1,1,128]{3,2,1,0:T(1,128)}, f32[3,3]{1,0:T(4,128)}) custom-call(f32[8,128]{1,0:T(8,128)S(1)} %ewald.1.result), custom_call_target="tpu_custom_call" | custom-call | tf_op jit(solution)/shard_map/hand_over/pallas_call | solution.py:660

commit v6 on v5

--- a/solution.py
+++ b/solution.py
@@ -301,7 +301,7 @@
         kinds[pl.ds(at, 8), :] = jnp.where(rows8 + at < live, picked[3], -1.0)
         return carry
 
-    lax.fori_loop(0, 8, edge, 0, unroll=2)
+    lax.fori_loop(0, 8, edge, 0, unroll=4)
 
     def radial(r, rate):
         e = jnp.exp(dist[...] * (-rate))
@@ -314,7 +314,7 @@
         basis[pl.ds(pl.multiple_of(r * 8, 8), 8), :] = tile
         return rate * GROWTH
 
-    lax.fori_loop(0, BASIS, radial, jnp.float32(RATE), unroll=4)
+    lax.fori_loop(0, BASIS, radial, jnp.float32(RATE), unroll=8)
 
     aggregate = dot(basis[...], w2[...], 0, 0, HIGH)
     u = dot(aggregate, wmix[...], 1, 0, HIGH)
@@ -567,7 +567,7 @@
         return rate * GROWTH, grad + chosen * expo[r]
 
     _, slope = lax.fori_loop(
-        0, BASIS, radial_back, (jnp.float32(RATE), jnp.zeros((SLOTS, 128), F32)), unroll=4
+        0, BASIS, radial_back, (jnp.float32(RATE), jnp.zeros((SLOTS, 128), F32)), unroll=8
     )
     spent = []
     for d in range(3):

time: 58.7 us -> 58.5 us (level)
  no operation moved by 1% of the time
where the time goes in v6:
time: 58.5 us; the launch traced here: 58.4 us
  Pallas kernels  57.8 us (99%)
  between operations  0.64 us (1%)
    pallas_call x1, Pallas kernels, per_device(): pl.pallas_call(kernel, out_shape=pltpu.VMEM((8, 128), F32), in_specs=[pl....  57.1 us

profile of v6, /device:TPU:1, one launch (start us, length us, event | category | flops | bytes accessed | tf_op | source)
XLA Modules:
  0.0 58.4 jit_solution(1761031002638751813)
XLA Ops:
  0.6 57.1 %ewald.1.result = f32[8,128]{1,0:T(8,128)S(1)} custom-call(f32[3,1,1,128]{3,2,1,0:T(1,128)} %refs_0_.1, s32[1,1,128]{2,1,0:T(1,128)} %refs_1_.1, s32[1,1,128]{2,1,0:T(1,128)} %refs_2_.1, s32[1,1,64,128]{3,2,1,0:T(8,128)} %refs_3_.1, s32[1,1,8,128]{3,2,1,0:T(8,128)} %refs_4_.1, s32[3,1000]{1,0:T(4,128)} %refs_5_.1, f32[6,128]{1,0:T(8,128)} %refs_6_.1, ...), custom_call_target="tpu_custom_call" | custom-call | tf_op jit(solution)/shard_map/ewald/pallas_call | solution.py:641
  57.8 0.7 %hand_over.1 = (f32[3,1,1,128]{3,2,1,0:T(1,128)}, f32[3,3]{1,0:T(4,128)}) custom-call(f32[8,128]{1,0:T(8,128)S(1)} %ewald.1.result), custom_call_target="tpu_custom_call" | custom-call | tf_op jit(solution)/shard_map/hand_over/pallas_call | solution.py:660
